TPU v7x, 32 devices: a whole 2x2x4 slice. The times are simulated.
32 devices in a mesh: section: 2 (over core), ctx: 8 (over z, x), tp: 2 (over y).
Axes of the slice: x: 2, y: 2, z: 4, core: 2. Of those that a mesh axis runs over, the one named last changes fastest.
Arguments:
- layer_input: bfloat16 [2, 1024, 1024], P(None, 'ctx'), may hold values from -6 to 6
- cotangent: bfloat16 [2, 1024, 1024], P(None, 'ctx'), may hold values from -6 to 6
- w_qkv: bfloat16 [2, 1024, 3, 1024], P('section', None, None, 'tp'), may hold values from -0.1875 to 0.1875
- b_qv: bfloat16 [2, 2, 1024], P('section', None, 'tp'), may hold values from -3 to 3
- w_out: bfloat16 [2, 1024, 1024], P('section', 'tp'), may hold values from -4 to 4
- b_out: bfloat16 [2, 1024], P('section'), may hold values from -3 to 3
- w_fc: bfloat16 [2, 1024, 4096], P('section', None, 'tp'), may hold values from -0.1875 to 0.1875
- b_fc: bfloat16 [2, 4096], P('section', 'tp'), may hold values from -3 to 3
- w_proj: bfloat16 [2, 4096, 1024], P('section', 'tp'), may hold values from -0.09375 to 0.09375
- b_proj: bfloat16 [2, 1024], P('section'), may hold values from -3 to 3
- ln_gain: float32 [2, 2, 1024], P('section'), may hold values from 0.5 to 1.5
- ln_bias: float32 [2, 2, 1024], P('section'), may hold values from -3 to 3
Outputs:
- activations: bfloat16 [2, 2, 1024, 1024], P('section', None, 'ctx')
- input_grads: float32 [2, 2, 1024, 1024], P('section', None, 'ctx')
- grad_w_qkv: float32 [2, 1024, 3, 1024], P('section', None, None, 'tp')
- grad_b_qv: float32 [2, 2, 1024], P('section', None, 'tp')
- grad_w_out: float32 [2, 1024, 1024], P('section', 'tp')
- grad_b_out: float32 [2, 1024], P('section')
- grad_w_fc: float32 [2, 1024, 4096], P('section', None, 'tp')
- grad_b_fc: float32 [2, 4096], P('section', 'tp')
- grad_w_proj: float32 [2, 4096, 1024], P('section', 'tp')
- grad_b_proj: float32 [2, 1024], P('section')
- grad_ln_gain: float32 [2, 2, 1024], P('section')
- grad_ln_bias: float32 [2, 2, 1024], P('section')
All inputs are finite; a program needn't handle non-finite values.
Results may differ from a plain program's by a relative error of at most 0.028.
Values may be sent and summed in bfloat16 or wider, within the bound.
A program may use at most 192 MiB of HBM per device.

v0:
```python
import jax
import jax.numpy as jnp
from jax import lax
from jax.sharding import PartitionSpec as P

HD = 64


EPS = 1e-05
GELU_C = 0.7978845608028654


def shifted(value, axis, steps):
    count = lax.axis_size(axis)
    first, last = (max(0, -steps), min(count, count - steps))
    return lax.ppermute(value, axis, [(source, source + steps) for source in range(first, last)])


def norm_forward(values, gain_vec, shift_vec):
    row_mean = jnp.mean(values, axis=-1, keepdims=True)
    centered = values - row_mean
    inv_std = lax.rsqrt(jnp.mean(centered * centered, axis=-1, keepdims=True) + EPS)
    normed = centered * inv_std
    return (normed * gain_vec + shift_vec, normed, inv_std)


def norm_backward(upstream, normed, inv_std, gain_vec):
    dnormed = upstream * gain_vec
    centered_grad = (
        dnormed
        - jnp.mean(dnormed, axis=-1, keepdims=True)
        - normed * jnp.mean(dnormed * normed, axis=-1, keepdims=True)
    )
    return (inv_std * centered_grad, jnp.sum(upstream * normed, axis=0), jnp.sum(upstream, axis=0))


def gelu_parts(pre_act):
    tanh_val = jnp.tanh(GELU_C * (pre_act + 0.044715 * pre_act * pre_act * pre_act))
    gelu_value = 0.5 * pre_act * (1.0 + tanh_val)
    gelu_slope = 0.5 * (1.0 + tanh_val) + 0.5 * pre_act * (1.0 - tanh_val * tanh_val) * GELU_C * (
        1.0 + 3.0 * 0.044715 * pre_act * pre_act
    )
    return (gelu_value, gelu_slope)


def split_heads(values, head_count):
    return values.reshape(values.shape[0], head_count, values.shape[1] // head_count)


def fold_keys(running, block_kv, queries, query_pos, head_count):
    totals, accum = running
    key_rows, val_rows = block_kv
    head_q = split_heads(queries, head_count)
    head_k = split_heads(key_rows, head_count)
    head_v = split_heads(val_rows, head_count)
    score_scale = HD ** (-0.5)
    scores = (
        jnp.einsum("qhd,khd->hqk", head_q, head_k, preferred_element_type=jnp.float32) * score_scale
    )
    key_pos = jnp.arange(key_rows.shape[0], dtype=jnp.int32)
    causal = query_pos[:, None] >= key_pos[None, :]
    weights = jnp.where(causal[None], jnp.exp(scores), 0.0)
    totals = jnp.sum(weights, axis=-1).T
    portion = jnp.einsum(
        "hqk,khd->qhd", weights.astype(jnp.bfloat16), head_v, preferred_element_type=jnp.float32
    )
    return (totals, portion.reshape(accum.shape))


def layer_forward(layer_in, weights_set, query_pos):
    w_qkv, b_qv, w_out, b_out, w_fc, b_fc, w_proj, b_proj, ln_gain, ln_bias = weights_set
    row_count, model_width = layer_in.shape
    local_cols = w_qkv.shape[2]
    head_count = local_cols // HD
    layer_f32 = layer_in.astype(jnp.float32)
    first_norm, normed_a, inv_a = norm_forward(layer_f32, ln_gain[0], ln_bias[0])
    first_bf = first_norm.astype(jnp.bfloat16)
    joined = jnp.dot(
        first_bf, w_qkv.reshape(model_width, 3 * local_cols), preferred_element_type=jnp.float32
    )
    queries = (joined[:, :local_cols] + b_qv[0].astype(jnp.float32)).astype(jnp.bfloat16)
    key_rows = joined[:, local_cols : 2 * local_cols].astype(jnp.bfloat16)
    val_rows = (joined[:, 2 * local_cols :] + b_qv[1].astype(jnp.float32)).astype(jnp.bfloat16)
    init_state = (
        jnp.zeros((row_count, head_count), jnp.float32),
        jnp.zeros((row_count, local_cols), jnp.float32),
    )
    totals, accum = fold_keys(
        init_state,
        (
            lax.all_gather(key_rows, "ctx", axis=0, tiled=True),
            lax.all_gather(val_rows, "ctx", axis=0, tiled=True),
        ),
        queries,
        query_pos,
        head_count,
    )
    held_keys = (key_rows, val_rows)
    attended = (
        (accum.reshape(row_count, head_count, HD) / totals[:, :, None])
        .reshape(row_count, local_cols)
        .astype(jnp.bfloat16)
    )
    log_total = jnp.log(totals)
    attn_mixed = lax.psum(
        jnp.dot(attended, w_out, preferred_element_type=jnp.float32).astype(jnp.bfloat16), "tp"
    ).astype(jnp.float32)
    hidden_in = layer_f32 + attn_mixed + b_out.astype(jnp.float32)
    second_norm, normed_b, inv_b = norm_forward(hidden_in, ln_gain[1], ln_bias[1])
    second_bf = second_norm.astype(jnp.bfloat16)
    pre_act = jnp.dot(second_bf, w_fc, preferred_element_type=jnp.float32) + b_fc.astype(
        jnp.float32
    )
    gelu_value, gelu_slope = gelu_parts(pre_act)
    act_bf = gelu_value.astype(jnp.bfloat16)
    mlp_mixed = lax.psum(
        jnp.dot(act_bf, w_proj, preferred_element_type=jnp.float32).astype(jnp.bfloat16), "tp"
    ).astype(jnp.float32)
    result = hidden_in + mlp_mixed + b_proj.astype(jnp.float32)
    saved = (
        normed_a,
        inv_a,
        first_bf,
        queries,
        (key_rows, val_rows),
        held_keys,
        attended,
        log_total,
        normed_b,
        inv_b,
        second_bf,
        act_bf,
        gelu_slope,
    )
    return (result.astype(jnp.bfloat16), saved)


def layer_backward(upstream, saved, weights_set, query_pos):
    w_qkv, b_qv, w_out, b_out, w_fc, b_fc, w_proj, b_proj, ln_gain, ln_bias = weights_set
    (
        normed_a,
        inv_a,
        first_bf,
        queries,
        own_kv,
        held_keys,
        attended,
        log_total,
        normed_b,
        inv_b,
        second_bf,
        act_bf,
        gelu_slope,
    ) = saved
    row_count, model_width = upstream.shape
    local_cols = w_qkv.shape[2]
    head_count = local_cols // HD
    score_scale = HD ** (-0.5)
    up_bf = upstream.astype(jnp.bfloat16)
    grad_b_proj = jnp.sum(upstream, axis=0)
    grad_w_proj = jnp.dot(act_bf.T, up_bf, preferred_element_type=jnp.float32)
    d_pre = jnp.dot(up_bf, w_proj.T, preferred_element_type=jnp.float32) * gelu_slope
    d_pre_bf = d_pre.astype(jnp.bfloat16)
    grad_b_fc = jnp.sum(d_pre, axis=0)
    grad_w_fc = jnp.dot(second_bf.T, d_pre_bf, preferred_element_type=jnp.float32)
    d_second = lax.psum(
        jnp.dot(d_pre_bf, w_fc.T, preferred_element_type=jnp.float32).astype(jnp.bfloat16), "tp"
    ).astype(jnp.float32)
    d_hidden_ln, gain_b, shift_b = norm_backward(d_second, normed_b, inv_b, ln_gain[1])
    d_hidden = upstream + d_hidden_ln
    grad_b_out = jnp.sum(d_hidden, axis=0)
    hidden_bf = d_hidden.astype(jnp.bfloat16)
    grad_w_out = jnp.dot(attended.T, hidden_bf, preferred_element_type=jnp.float32)
    d_attended = jnp.dot(hidden_bf, w_out.T, preferred_element_type=jnp.float32).astype(
        jnp.bfloat16
    )
    all_keys, all_vals = (
        lax.all_gather(held_keys[0], "ctx", axis=0, tiled=True),
        lax.all_gather(held_keys[1], "ctx", axis=0, tiled=True),
    )
    head_q = split_heads(queries, head_count)
    head_k = split_heads(all_keys, head_count)
    head_v = split_heads(all_vals, head_count)
    head_d = split_heads(d_attended, head_count)
    scores = (
        jnp.einsum("qhd,khd->hqk", head_q, head_k, preferred_element_type=jnp.float32) * score_scale
    )
    key_pos = jnp.arange(all_keys.shape[0], dtype=jnp.int32)
    causal = query_pos[:, None] >= key_pos[None, :]
    probs = jnp.where(causal[None], jnp.exp(scores - log_total.T[:, :, None]), 0.0)
    row_delta = jnp.sum(
        d_attended.astype(jnp.float32).reshape(row_count, head_count, HD)
        * attended.astype(jnp.float32).reshape(row_count, head_count, HD),
        axis=-1,
    )
    d_probs = jnp.einsum("qhd,khd->hqk", head_d, head_v, preferred_element_type=jnp.float32)
    d_scores = (probs * (d_probs - row_delta.T[:, :, None])).astype(jnp.bfloat16)
    d_query = (
        jnp.einsum("hqk,khd->qhd", d_scores, head_k, preferred_element_type=jnp.float32).reshape(
            row_count, local_cols
        )
        * score_scale
    )
    key_term = (
        jnp.einsum("hqk,qhd->khd", d_scores, head_q, preferred_element_type=jnp.float32).reshape(
            all_keys.shape[0], local_cols
        )
        * score_scale
    )
    val_term = jnp.einsum(
        "hqk,qhd->khd", probs.astype(jnp.bfloat16), head_d, preferred_element_type=jnp.float32
    ).reshape(all_keys.shape[0], local_cols)
    d_key, d_val = (
        lax.psum_scatter(
            key_term.astype(jnp.bfloat16), "ctx", scatter_dimension=0, tiled=True
        ).astype(jnp.float32),
        lax.psum_scatter(
            val_term.astype(jnp.bfloat16), "ctx", scatter_dimension=0, tiled=True
        ).astype(jnp.float32),
    )
    grad_b_qv = jnp.stack([jnp.sum(d_query, axis=0), jnp.sum(d_val, axis=0)])
    d_joined = jnp.concatenate([d_query, d_key, d_val], axis=1).astype(jnp.bfloat16)
    grad_w_qkv = jnp.dot(first_bf.T, d_joined, preferred_element_type=jnp.float32).reshape(
        model_width, 3, local_cols
    )
    d_first = lax.psum(
        jnp.dot(
            d_joined,
            w_qkv.reshape(model_width, 3 * local_cols).T,
            preferred_element_type=jnp.float32,
        ).astype(jnp.bfloat16),
        "tp",
    ).astype(jnp.float32)
    d_in_ln, gain_a, shift_a = norm_backward(d_first, normed_a, inv_a, ln_gain[0])
    d_input = d_hidden + d_in_ln
    grads = (
        grad_w_qkv,
        grad_b_qv,
        grad_w_out,
        grad_b_out,
        grad_w_fc,
        grad_b_fc,
        grad_w_proj,
        grad_b_proj,
        jnp.stack([gain_a, gain_b]),
        jnp.stack([shift_a, shift_b]),
    )
    return (d_input, grads)


def body(
    layer_input, cotangent, w_qkv, b_qv, w_out, b_out, w_fc, b_fc, w_proj, b_proj, ln_gain, ln_bias
):
    weights_set = (
        w_qkv[0],
        b_qv[0],
        w_out[0],
        b_out[0],
        w_fc[0],
        b_fc[0],
        w_proj[0],
        b_proj[0],
        ln_gain[0],
        ln_bias[0],
    )
    later_segment = lax.axis_index("section") == 1
    micro, row_count, model_width = layer_input.shape
    query_pos = lax.axis_index("ctx") * row_count + jnp.arange(row_count, dtype=jnp.int32)
    incoming = jnp.zeros((row_count, model_width), jnp.bfloat16)
    results = []
    saved_ticks = []
    for tick_index in range(micro + 1):
        if tick_index < micro:
            fresh_input = layer_input[tick_index]
        else:
            fresh_input = jnp.zeros((row_count, model_width), jnp.bfloat16)
        layer_in = jnp.where(later_segment, incoming, fresh_input)
        result, saved = layer_forward(layer_in, weights_set, query_pos)
        results.append(result)
        saved_ticks.append(saved)
        if tick_index < micro:
            incoming = shifted(result, "section", 1)
    outgoing = jnp.zeros((row_count, model_width), jnp.float32)
    grad_totals = []
    input_grads_all = []
    for tick_index in range(micro + 1):
        if tick_index < micro:
            given_grad = cotangent[tick_index].astype(jnp.float32)
        else:
            given_grad = jnp.zeros((row_count, model_width), jnp.float32)
        upstream = jnp.where(later_segment, given_grad, outgoing)
        saved = jax.tree.map(
            lambda late_val, early_val: jnp.where(later_segment, late_val, early_val),
            saved_ticks[min(tick_index + 1, micro)],
            saved_ticks[max(tick_index - 1, 0)],
        )
        d_input, grads = layer_backward(upstream, saved, weights_set, query_pos)
        if tick_index == 0:
            grad_totals = grads
        else:
            grad_totals = jax.tree.map(jnp.add, grad_totals, grads)
        input_grads_all.append(d_input)
        if tick_index < micro:
            outgoing = shifted(d_input.astype(jnp.bfloat16), "section", -1).astype(d_input.dtype)
    activations = jnp.stack(
        [
            jnp.where(later_segment, results[batch_index + 1], results[batch_index])
            for batch_index in range(micro)
        ]
    )[None]
    input_grads = jnp.stack(
        [
            jnp.where(later_segment, input_grads_all[batch_index], input_grads_all[batch_index + 1])
            for batch_index in range(micro)
        ]
    )[None]
    summed = (
        lax.psum(grad_totals[0].astype(jnp.bfloat16), "ctx").astype(jnp.float32),
        lax.psum(grad_totals[1].astype(jnp.bfloat16), "ctx").astype(jnp.float32),
        lax.psum(grad_totals[2].astype(jnp.bfloat16), "ctx").astype(jnp.float32),
        lax.psum(grad_totals[3].astype(jnp.bfloat16), "ctx").astype(jnp.float32),
        lax.psum(grad_totals[4].astype(jnp.bfloat16), "ctx").astype(jnp.float32),
        lax.psum(grad_totals[5].astype(jnp.bfloat16), "ctx").astype(jnp.float32),
        lax.psum(grad_totals[6].astype(jnp.bfloat16), "ctx").astype(jnp.float32),
        lax.psum(grad_totals[7].astype(jnp.bfloat16), "ctx").astype(jnp.float32),
        lax.psum(grad_totals[8].astype(jnp.bfloat16), "ctx").astype(jnp.float32),
        lax.psum(grad_totals[9].astype(jnp.bfloat16), "ctx").astype(jnp.float32),
    )
    return (
        activations,
        input_grads,
        summed[0][None],
        summed[1][None],
        summed[2][None],
        summed[3][None],
        summed[4][None],
        summed[5][None],
        summed[6][None],
        summed[7][None],
        summed[8][None],
        summed[9][None],
    )


def solution(mesh):
    placed = (
        P(None, "ctx", None),
        P(None, "ctx", None),
        P("section", None, None, "tp"),
        P("section", None, "tp"),
        P("section", "tp", None),
        P("section", None),
        P("section", None, "tp"),
        P("section", "tp"),
        P("section", "tp", None),
        P("section", None),
        P("section", None, None),
        P("section", None, None),
    )
    return jax.shard_map(
        body,
        mesh=mesh,
        in_specs=placed,
        out_specs=(
            P("section", None, "ctx", None),
            P("section", None, "ctx", None),
            P("section", None, None, "tp"),
            P("section", None, "tp"),
            P("section", "tp", None),
            P("section", None),
            P("section", None, "tp"),
            P("section", "tp"),
            P("section", "tp", None),
            P("section", None),
            P("section", None, None),
            P("section", None, None),
        ),
        check_vma=False,
    )
```

profile of v0, /device:TPU:1, one launch (start us, length us, event | category | flops | bytes accessed | tf_op | source)
XLA Modules:
  0.0 1655.1 jit_solution(18073447266085569030)
XLA Ops:
  21.0 39.6 %all-gather.15.cloned.1.call-done = bf16[1024,512]{1,0:T(8,128)(2,1)} async-done(((bf16[128,512]{1,0:T(8,128)(2,1)}), bf16[1024,512]{1,0:T(8,128)(2,1)}) %all-gather.15.cloned.1.call-update) | async-done | bytes 1048592 | tf_op jit(solution)/shard_map/all_gather | solution.py:91
  67.3 34.5 %all-gather.13.cloned.1.call-done = bf16[1024,512]{1,0:T(8,128)(2,1)} async-done(((bf16[128,512]{1,0:T(8,128)(2,1)}), bf16[1024,512]{1,0:T(8,128)(2,1)}) %all-gather.13.cloned.1.call-update) | async-done | bytes 1048592 | tf_op jit(solution)/shard_map/all_gather | solution.py:92
  107.5 23.2 %all-reduce.16.cloned.1.call-done = bf16[128,1024]{1,0:T(8,128)(2,1)} async-done(((bf16[128,1024]{1,0:T(8,128)(2,1)}), bf16[128,1024]{1,0:T(8,128)(2,1)}) %all-reduce.16.cloned.1.call-update) | async-done | bytes 262160 | tf_op jit(solution)/shard_map/psum | solution.py:105
  138.3 23.4 %all-reduce.18.cloned.1.call-done = bf16[128,1024]{1,0:T(8,128)(2,1)} async-done(((bf16[128,1024]{1,0:T(8,128)(2,1)}), bf16[128,1024]{1,0:T(8,128)(2,1)}) %all-reduce.18.cloned.1.call-update) | async-done | bytes 262160 | tf_op jit(solution)/shard_map/psum | solution.py:116
  173.5 37.5 %all-gather.19.cloned.1.call-done = bf16[1024,512]{1,0:T(8,128)(2,1)} async-done(((bf16[128,512]{1,0:T(8,128)(2,1)}), bf16[1024,512]{1,0:T(8,128)(2,1)}) %all-gather.19.cloned.1.call-update) | async-done | bytes 1048592 | tf_op jit(solution)/shard_map/all_gather | solution.py:91
  218.2 33.7 %all-gather.17.cloned.1.call-done = bf16[1024,512]{1,0:T(8,128)(2,1)} async-done(((bf16[128,512]{1,0:T(8,128)(2,1)}), bf16[1024,512]{1,0:T(8,128)(2,1)}) %all-gather.17.cloned.1.call-update) | async-done | bytes 1048592 | tf_op jit(solution)/shard_map/all_gather | solution.py:92
  258.9 23.1 %all-reduce.20.cloned.1.call-done = bf16[128,1024]{1,0:T(8,128)(2,1)} async-done(((bf16[128,1024]{1,0:T(8,128)(2,1)}), bf16[128,1024]{1,0:T(8,128)(2,1)}) %all-reduce.20.cloned.1.call-update) | async-done | bytes 262160 | tf_op jit(solution)/shard_map/psum | solution.py:105
  296.7 28.4 %all-reduce.34.cloned.1.call-done = (bf16[128,1024]{1,0:T(8,128)(2,1)}, bf16[128,1024]{1,0:T(8,128)(2,1)}) async-done(((bf16[128,1024]{1,0:T(8,128)(2,1)}, bf16[128,1024]{1,0:T(8,128)(2,1)}), (bf16[128,1024]{1,0:T(8,128)(2,1)}, bf16[128,1024]{1,0:T(8,128)(2,1)})) %all-reduce.34.cloned.1.call-update) | async-done | bytes 524304 | tf_op jit(solution)/shard_map/psum | solution.py:166
  338.3 28.2 %all-gather.25.cloned.1.call-done = bf16[1024,512]{1,0:T(8,128)(2,1)} async-done(((bf16[128,512]{1,0:T(8,128)(2,1)}), bf16[1024,512]{1,0:T(8,128)(2,1)}) %all-gather.25.cloned.1.call-update) | async-done | bytes 1048592 | tf_op jit(solution)/shard_map/all_gather | solution.py:178
  379.4 28.2 %all-gather.23.cloned.1.call-done = bf16[1024,512]{1,0:T(8,128)(2,1)} async-done(((bf16[128,512]{1,0:T(8,128)(2,1)}), bf16[1024,512]{1,0:T(8,128)(2,1)}) %all-gather.23.cloned.1.call-update) | async-done | bytes 1048592 | tf_op jit(solution)/shard_map/all_gather | solution.py:91
  419.8 28.9 %all-gather.27.cloned.1.call-done = bf16[1024,512]{1,0:T(8,128)(2,1)} async-done(((bf16[128,512]{1,0:T(8,128)(2,1)}), bf16[1024,512]{1,0:T(8,128)(2,1)}) %all-gather.27.cloned.1.call-update) | async-done | bytes 1048592 | tf_op jit(solution)/shard_map/all_gather | solution.py:179
  461.9 27.8 %all-gather.21.cloned.1.call-done = bf16[1024,512]{1,0:T(8,128)(2,1)} async-done(((bf16[128,512]{1,0:T(8,128)(2,1)}), bf16[1024,512]{1,0:T(8,128)(2,1)}) %all-gather.21.cloned.1.call-update) | async-done | bytes 1048592 | tf_op jit(solution)/shard_map/all_gather | solution.py:92
  498.1 58.5 %reduce-scatter.21.cloned.1.call-done = bf16[128,512]{1,0:T(8,128)(2,1)} async-done(((bf16[1024,512]{1,0:T(8,128)(2,1)}), bf16[128,512]{1,0:T(8,128)(2,1)}) %reduce-scatter.21.cloned.1.call-update) | async-done | bytes 131088
  557.6 65.4 %reduce-scatter.19.cloned.1.call-done = bf16[128,512]{1,0:T(8,128)(2,1)} async-done(((bf16[1024,512]{1,0:T(8,128)(2,1)}), bf16[128,512]{1,0:T(8,128)(2,1)}) %reduce-scatter.19.cloned.1.call-update) | async-done | bytes 131088
  629.2 27.6 %all-reduce.32.cloned.1.call-done = (bf16[128,1024]{1,0:T(8,128)(2,1)}, bf16[128,1024]{1,0:T(8,128)(2,1)}) async-done(((bf16[128,1024]{1,0:T(8,128)(2,1)}, bf16[128,1024]{1,0:T(8,128)(2,1)}), (bf16[128,1024]{1,0:T(8,128)(2,1)}, bf16[128,1024]{1,0:T(8,128)(2,1)})) %all-reduce.32.cloned.1.call-update) | async-done | bytes 524304 | tf_op jit(solution)/shard_map/psum | solution.py:226
  680.0 18.1 %all-gather.29.cloned.1.call-done = bf16[1024,512]{1,0:T(8,128)(2,1)} async-done(((bf16[128,512]{1,0:T(8,128)(2,1)}), bf16[1024,512]{1,0:T(8,128)(2,1)}) %all-gather.29.cloned.1.call-update) | async-done | bytes 1048592 | tf_op jit(solution)/shard_map/all_gather | solution.py:178
  704.3 19.7 %all-reduce.22.cloned.1.call-done = bf16[128,1024]{1,0:T(8,128)(2,1)} async-done(((bf16[128,1024]{1,0:T(8,128)(2,1)}), bf16[128,1024]{1,0:T(8,128)(2,1)}) %all-reduce.22.cloned.1.call-update) | async-done | bytes 262160 | tf_op jit(solution)/shard_map/psum | solution.py:166
  737.5 27.6 %all-gather.31.cloned.1.call-done = bf16[1024,512]{1,0:T(8,128)(2,1)} async-done(((bf16[128,512]{1,0:T(8,128)(2,1)}), bf16[1024,512]{1,0:T(8,128)(2,1)}) %all-gather.31.cloned.1.call-update) | async-done | bytes 1048592 | tf_op jit(solution)/shard_map/all_gather | solution.py:179
  792.8 13.4 all-gather.33.cloned.1.call-done
  808.5 38.7 %all-gather.35.cloned.1.call-done = bf16[1024,512]{1,0:T(8,128)(2,1)} async-done(((bf16[128,512]{1,0:T(8,128)(2,1)}), bf16[1024,512]{1,0:T(8,128)(2,1)}) %all-gather.35.cloned.1.call-update) | async-done | bytes 1048592 | tf_op jit(solution)/shard_map/all_gather | solution.py:179
  855.9 57.6 %reduce-scatter.25.cloned.1.call-done = bf16[128,512]{1,0:T(8,128)(2,1)} async-done(((bf16[1024,512]{1,0:T(8,128)(2,1)}), bf16[128,512]{1,0:T(8,128)(2,1)}) %reduce-scatter.25.cloned.1.call-update) | async-done | bytes 131088
  915.2 65.0 %reduce-scatter.23.cloned.1.call-done = bf16[128,512]{1,0:T(8,128)(2,1)} async-done(((bf16[1024,512]{1,0:T(8,128)(2,1)}), bf16[128,512]{1,0:T(8,128)(2,1)}) %reduce-scatter.23.cloned.1.call-update) | async-done | bytes 131088
  990.4 18.6 %all-reduce.24.cloned.1.call-done = bf16[128,1024]{1,0:T(8,128)(2,1)} async-done(((bf16[128,1024]{1,0:T(8,128)(2,1)}), bf16[128,1024]{1,0:T(8,128)(2,1)}) %all-reduce.24.cloned.1.call-update) | async-done | bytes 262160 | tf_op jit(solution)/shard_map/psum | solution.py:226
  1034.0 15.8 all-reduce.26.cloned.1.call-done
  1083.4 9.6 fusion.30
  1093.0 9.2 fusion.31
  1106.0 21.1 %reduce-scatter.29.cloned.1.call-done = bf16[128,512]{1,0:T(8,128)(2,1)} async-done(((bf16[1024,512]{1,0:T(8,128)(2,1)}), bf16[128,512]{1,0:T(8,128)(2,1)}) %reduce-scatter.29.cloned.1.call-update) | async-done | bytes 131088
  1128.2 65.4 %reduce-scatter.27.cloned.1.call-done = bf16[128,512]{1,0:T(8,128)(2,1)} async-done(((bf16[1024,512]{1,0:T(8,128)(2,1)}), bf16[128,512]{1,0:T(8,128)(2,1)}) %reduce-scatter.27.cloned.1.call-update) | async-done | bytes 131088
  1198.0 7.5 add_convert_fusion.2
  1220.4 6.9 all-reduce.30.cloned.1.call-done
  1230.1 32.1 %all-reduce = (bf16[1,2,512]{2,1,0:T(2,128)(2,1)S(1)}, bf16[1,1024]{1,0:T(2,128)(2,1)S(1)}, bf16[1,2048]{1,0:T(2,128)(2,1)S(1)}, bf16[1,1024]{1,0:T(2,128)(2,1)S...) all-reduce(bf16[1,2,512]{2,1,0:T(2,128)(2,1)S(1)} %fusion.327, ...), channel_id=1, replica_groups=mesh['section'=2,'ctx'=8,'tp'=2] {'ctx'}, use_global_device_ids=true, to_apply=%region_55.56 | all-reduce | flops 9216 | bytes 36864 | tf_op jit(solution)/shard_map/psum | solution.py:319
  1271.1 357.3 %all-reduce.28.cloned.1.call-done = (bf16[1,1024,3,512]{1,3,2,0:T(8,128)(2,1)}, bf16[1,512,1024]{2,1,0:T(8,128)(2,1)}, bf16[1,1024,2048]{2,1,0:T(8,128)(2,1)}, bf16[1,2048,1024]{2,1,0:T(8,128)(2,1)}) async-done(((bf16[1,1024,3,512]{1,3,2,0:T(8,128)(2,1)}, bf16[1,512,1024]{2,1,0:T(8,128)(2,1)}, bf16[1,1024,2048]{2,1,0:T(8,128)(2,1)}, bf16[1,2048,1024]{2,1,0:T(8,128)(2,1)}), ...) | async-done | bytes 12582928 | tf_op jit(solution)/shard_map/psum | solution.py:318
  (557 shorter events, 346.9 us)
Async XLA Ops:
  7.2 53.4 %all-gather.15.cloned.1.call-start = ((), (), s32[]{:S(2)}) async-start(), calls=%async_computation.7 | async-start | bytes 1179648 | tf_op jit(solution)/shard_map/all_gather | solution.py:91
  19.8 81.9 %all-gather.13.cloned.1.call-start = ((), (), s32[]{:S(2)}) async-start(), calls=%async_computation.6 | async-start | bytes 1179648 | tf_op jit(solution)/shard_map/all_gather | solution.py:92
  20.6 110.2 %all-reduce.16.cloned.1.call-start = ((), (), s32[]{:S(2)}) async-start(), calls=%async_computation.8 | async-start | bytes 524288 | tf_op jit(solution)/shard_map/psum | solution.py:105
  107.4 54.2 %all-reduce.18.cloned.1.call-start = ((), (), s32[]{:S(2)}) async-start(), calls=%async_computation.9 | async-start | bytes 524288 | tf_op jit(solution)/shard_map/psum | solution.py:116
  138.2 72.7 %all-gather.19.cloned.1.call-start = ((), (), s32[]{:S(2)}) async-start(), calls=%async_computation.11 | async-start | bytes 1179648 | tf_op jit(solution)/shard_map/all_gather | solution.py:91
  162.8 3.5 collective-permute-start
  172.7 79.2 %all-gather.17.cloned.1.call-start = ((), (), s32[]{:S(2)}) async-start(), calls=%async_computation.10 | async-start | bytes 1179648 | tf_op jit(solution)/shard_map/all_gather | solution.py:92
  173.3 108.7 %all-reduce.20.cloned.1.call-start = ((), (), s32[]{:S(2)}) async-start(), calls=%async_computation.12 | async-start | bytes 524288 | tf_op jit(solution)/shard_map/psum | solution.py:105
  258.7 66.4 %all-reduce.34.cloned.1.call-start = ((), (), s32[]{:S(2)}) async-start(), calls=%async_computation.33 | async-start | bytes 1048576 | tf_op jit(solution)/shard_map/psum | solution.py:166
  295.9 70.6 %all-gather.25.cloned.1.call-start = ((), (), s32[]{:S(2)}) async-start(), calls=%async_computation.15 | async-start | bytes 1179648 | tf_op jit(solution)/shard_map/all_gather | solution.py:178
  296.6 110.9 %all-gather.23.cloned.1.call-start = ((), (), s32[]{:S(2)}) async-start(), calls=%async_computation.14 | async-start | bytes 1179648 | tf_op jit(solution)/shard_map/all_gather | solution.py:91
  326.9 3.4 collective-permute-start.1
  336.5 112.2 %all-gather.27.cloned.1.call-start = ((), (), s32[]{:S(2)}) async-start(), calls=%async_computation.16 | async-start | bytes 1179648 | tf_op jit(solution)/shard_map/all_gather | solution.py:179
  337.2 152.5 %all-gather.21.cloned.1.call-start = ((), (), s32[]{:S(2)}) async-start(), calls=%async_computation.13 | async-start | bytes 1179648 | tf_op jit(solution)/shard_map/all_gather | solution.py:92
  372.8 183.7 %reduce-scatter.21.cloned.1.call-start = ((), (), s32[]{:S(2)}) async-start(), calls=%async_computation.25 | async-start | bytes 1179648
  419.5 203.5 %reduce-scatter.19.cloned.1.call-start = ((), (), s32[]{:S(2)}) async-start(), calls=%async_computation.24 | async-start | bytes 1179648
  461.8 194.9 %all-reduce.32.cloned.1.call-start = ((), (), s32[]{:S(2)}) async-start(), calls=%async_computation.32 | async-start | bytes 1048576 | tf_op jit(solution)/shard_map/psum | solution.py:226
  627.3 70.7 %all-gather.29.cloned.1.call-start = ((), (), s32[]{:S(2)}) async-start(), calls=%async_computation.18 | async-start | bytes 1179648 | tf_op jit(solution)/shard_map/all_gather | solution.py:178
  629.1 94.9 %all-reduce.22.cloned.1.call-start = ((), (), s32[]{:S(2)}) async-start(), calls=%async_computation.17 | async-start | bytes 524288 | tf_op jit(solution)/shard_map/psum | solution.py:166
  662.2 8.4 collective-permute-start.2
  676.0 89.1 %all-gather.31.cloned.1.call-start = ((), (), s32[]{:S(2)}) async-start(), calls=%async_computation.19 | async-start | bytes 1179648 | tf_op jit(solution)/shard_map/all_gather | solution.py:179
  677.6 128.6 %all-gather.33.cloned.1.call-start = ((), (), s32[]{:S(2)}) async-start(), calls=%async_computation.22 | async-start | bytes 1179648 | tf_op jit(solution)/shard_map/all_gather | solution.py:178
  678.4 168.8 %all-gather.35.cloned.1.call-start = ((), (), s32[]{:S(2)}) async-start(), calls=%async_computation.23 | async-start | bytes 1179648 | tf_op jit(solution)/shard_map/all_gather | solution.py:179
  679.5 234.0 %reduce-scatter.25.cloned.1.call-start = ((), (), s32[]{:S(2)}) async-start(), calls=%async_computation.27 | async-start | bytes 1179648
  737.5 242.7 %reduce-scatter.23.cloned.1.call-start = ((), (), s32[]{:S(2)}) async-start(), calls=%async_computation.26 | async-start | bytes 1179648
  778.3 230.7 %all-reduce.24.cloned.1.call-start = ((), (), s32[]{:S(2)}) async-start(), calls=%async_computation.20 | async-start | bytes 524288 | tf_op jit(solution)/shard_map/psum | solution.py:226
  985.2 64.6 %all-reduce.26.cloned.1.call-start = ((), (), s32[]{:S(2)}) async-start(), calls=%async_computation.21 | async-start | bytes 524288 | tf_op jit(solution)/shard_map/psum | solution.py:166
  1014.3 7.0 collective-permute-start.3
  1027.4 99.8 %reduce-scatter.29.cloned.1.call-start = ((), (), s32[]{:S(2)}) async-start(), calls=%async_computation.29 | async-start | bytes 1179648
  1063.9 129.7 %reduce-scatter.27.cloned.1.call-start = ((), (), s32[]{:S(2)}) async-start(), calls=%async_computation.28 | async-start | bytes 1179648
  1083.2 144.0 %all-reduce.30.cloned.1.call-start = ((), (), s32[]{:S(2)}) async-start(), calls=%async_computation.31 | async-start | bytes 1048576 | tf_op jit(solution)/shard_map/psum | solution.py:116
  1197.9 430.6 %all-reduce.28.cloned.1.call-start = ((), (), s32[]{:S(2)}) async-start(), calls=%async_computation.30 | async-start | bytes 25165824 | tf_op jit(solution)/shard_map/psum | solution.py:318
  (153 other events, 3741.8 us)
Sparse Core Ops, SparseCore 0:
  19.9 40.6 all-gather.14
  62.7 38.9 all-gather.12
  107.6 23.1 all-reduce.15
  138.3 23.2 all-reduce.17
  172.8 38.0 all-gather.18
  212.9 38.9 all-gather.16
  258.8 23.1 all-reduce.19
  296.0 28.9 all-reduce.33
  327.8 38.7 all-gather.24
  368.5 38.9 all-gather.22
  409.7 38.9 all-gather.26
  450.7 38.9 all-gather.20
  493.7 62.8 reduce-scatter.20
  559.8 63.1 reduce-scatter.18
  627.5 29.2 all-reduce.31
  659.3 38.7 all-gather.28
  700.8 23.1 all-reduce.21
  726.0 39.0 all-gather.30
  767.2 38.9 all-gather.32
  808.2 38.9 all-gather.34
  850.6 62.8 reduce-scatter.24
  916.9 63.2 reduce-scatter.22
  985.4 23.5 all-reduce.23
  1027.5 22.2 all-reduce.25
  1064.0 63.0 reduce-scatter.28
  1130.4 63.1 reduce-scatter.26
  1198.0 29.1 all-reduce.29
  1233.1 395.2 all-reduce.27
where the time goes:
time: 1670 us; the launch traced here: 1660 us
  waiting for transfers between devices  1240 us (74%)
  matrix products  188 us (11%)
  local copies, waits for them, and re-layouts  87.4 us (5%)
  other arithmetic  79.6 us (5%)
  blocking collectives  32.1 us (2%)
    psum x1, waiting for transfers between devices, body(): lax.psum(grad_totals[0].astype(jnp.bfloat16), 'ctx').astype(jnp.float32)  357 us
    unnamed x34, waiting for transfers between devices  336 us
    all_gather x3, waiting for transfers between devices, layer_forward(): lax.all_gather(key_rows, 'ctx', axis=0, tiled=True)  105 us
    all_gather x3, waiting for transfers between devices, layer_forward(): lax.all_gather(val_rows, 'ctx', axis=0, tiled=True)  96 us
    all_gather x3, waiting for transfers between devices, layer_backward(): lax.all_gather(held_keys[1], 'ctx', axis=0, tiled=True)  95.2 us
    psum x3, waiting for transfers between devices, layer_backward(): lax.psum(jnp.dot(d_pre_bf, w_fc.T, preferred_element_type=jnp.float32).as...  63.8 us
    all_gather x3, waiting for transfers between devices, layer_backward(): lax.all_gather(held_keys[0], 'ctx', axis=0, tiled=True)  59.7 us
    psum x2, waiting for transfers between devices, layer_forward(): lax.psum(jnp.dot(attended, w_out, preferred_element_type=jnp.float32).ast...  46.4 us
  transfers between devices with their start and end apart: 32, of which 30 were waited for; matrix products, arithmetic and copies ran while one was open for 14% of the time, Pallas kernels for 0%

commit v1 on v0

v1 whole, which is shorter than its diff:
```python
import functools

import jax
import jax.numpy as jnp
from jax import lax
from jax.experimental import pallas as pl
from jax.experimental.pallas import tpu as pltpu
from jax.sharding import PartitionSpec as P

HD = 64
EPS = 1e-05
GELU_C = 0.7978845608028654
F32 = jnp.float32
BF16 = jnp.bfloat16


def dot(lhs, rhs, lhs_dim, rhs_dim):
    return lax.dot_general(
        lhs, rhs, (((lhs_dim,), (rhs_dim,)), ((), ())), preferred_element_type=F32
    )


def norm_forward(values, gain_vec, shift_vec):
    row_mean = jnp.mean(values, axis=-1, keepdims=True)
    centered = values - row_mean
    inv_std = lax.rsqrt(jnp.mean(centered * centered, axis=-1, keepdims=True) + EPS)
    normed = centered * inv_std
    return (normed * gain_vec + shift_vec, normed, inv_std)


def norm_backward(upstream, normed, inv_std, gain_vec):
    dnormed = upstream * gain_vec
    centered_grad = (
        dnormed
        - jnp.mean(dnormed, axis=-1, keepdims=True)
        - normed * jnp.mean(dnormed * normed, axis=-1, keepdims=True)
    )
    return (inv_std * centered_grad, jnp.sum(upstream * normed, axis=0), jnp.sum(upstream, axis=0))


def gelu_parts(pre_act):
    tanh_val = jnp.tanh(GELU_C * (pre_act + 0.044715 * pre_act * pre_act * pre_act))
    gelu_value = 0.5 * pre_act * (1.0 + tanh_val)
    gelu_slope = 0.5 * (1.0 + tanh_val) + 0.5 * pre_act * (1.0 - tanh_val * tanh_val) * GELU_C * (
        1.0 + 3.0 * 0.044715 * pre_act * pre_act
    )
    return (gelu_value, gelu_slope)


def swap(value):
    return lax.ppermute(value, "section", [(0, 1), (1, 0)])


def tp_sum(part):
    part = part.astype(BF16)
    if lax.axis_size("tp") == 2:
        other = lax.ppermute(part, "tp", [(0, 1), (1, 0)])
        return part.astype(F32) + other.astype(F32)
    return lax.psum(part, "tp").astype(F32)


def a2a_kernel(n, x_ref, o_ref, send_sem, recv_sem, own_sem):
    me = lax.axis_index("ctx")
    barrier = pltpu.get_barrier_semaphore()
    for step in range(1, n):
        pl.semaphore_signal(
            barrier,
            inc=1,
            device_id={"ctx": lax.rem(me + step, n)},
            device_id_type=pl.DeviceIdType.MESH,
        )
    pl.semaphore_wait(barrier, n - 1)
    copies = []
    for step in range(1, n):
        peer = lax.rem(me + step, n)
        copy = pltpu.make_async_remote_copy(
            src_ref=x_ref.at[peer],
            dst_ref=o_ref.at[me],
            send_sem=send_sem.at[step],
            recv_sem=recv_sem.at[step],
            device_id={"ctx": peer},
            device_id_type=pl.DeviceIdType.MESH,
        )
        copy.start()
        copies.append(copy)
    own = pltpu.make_async_copy(x_ref.at[me], o_ref.at[me], own_sem)
    own.start()
    own.wait()
    for copy in copies:
        copy.wait()


def all_to_all(value, collective_id):
    n = value.shape[0]
    return pl.pallas_call(
        functools.partial(a2a_kernel, n),
        out_shape=jax.ShapeDtypeStruct(value.shape, value.dtype),
        in_specs=[pl.BlockSpec(memory_space=pltpu.VMEM)],
        out_specs=pl.BlockSpec(memory_space=pltpu.VMEM),
        scratch_shapes=[
            pltpu.SemaphoreType.DMA((n,)),
            pltpu.SemaphoreType.DMA((n,)),
            pltpu.SemaphoreType.DMA,
        ],
        compiler_params=pltpu.CompilerParams(collective_id=collective_id, has_side_effects=True),
        name="a2a",
    )(value)


def to_heads(value, collective_id):
    parts, cols, rows = value.shape
    n = lax.axis_size("ctx")
    sent = value.reshape(parts, n, cols // n, rows).transpose(1, 0, 2, 3)
    got = all_to_all(sent.reshape(n, parts * cols // n, rows), collective_id)
    got = got.reshape(n, parts, cols // n, rows).transpose(1, 2, 0, 3)
    return got.reshape(parts, cols // n // HD, HD, n * rows)


def to_tokens(value, collective_id):
    parts, heads, _, total = value.shape
    n = lax.axis_size("ctx")
    rows = total // n
    sent = value.reshape(parts, heads * HD, n, rows).transpose(2, 0, 1, 3)
    got = all_to_all(sent.reshape(n, parts * heads * HD, rows), collective_id)
    got = got.reshape(n, parts, heads * HD, rows).transpose(1, 0, 2, 3)
    return got.reshape(parts, n * heads * HD, rows)


def scores_of(queries, keys):
    return jnp.einsum("hdk,hdq->hkq", keys, queries, preferred_element_type=F32) * HD ** (-0.5)


def causal_of(query_pos, key_count):
    return (jnp.arange(key_count, dtype=jnp.int32)[:, None] <= query_pos[None, :])[None]


def attend(queries, keys, vals, query_pos):
    weights = jnp.where(
        causal_of(query_pos, keys.shape[2]), jnp.exp(scores_of(queries, keys)), 0.0
    )
    totals = jnp.sum(weights, axis=1)
    out = jnp.einsum("hdk,hkq->hdq", vals, weights.astype(BF16), preferred_element_type=F32)
    return (out / totals[:, None, :]).astype(BF16), jnp.log(totals)


def attend_backward(queries, keys, vals, attended, log_total, d_out, query_pos):
    probs = jnp.where(
        causal_of(query_pos, keys.shape[2]),
        jnp.exp(scores_of(queries, keys) - log_total[:, None, :]),
        0.0,
    )
    delta = jnp.sum(d_out.astype(F32) * attended.astype(F32), axis=1)
    d_probs = jnp.einsum("hdk,hdq->hkq", vals, d_out, preferred_element_type=F32)
    d_scores = (probs * (d_probs - delta[:, None, :])).astype(BF16)
    scale = HD ** (-0.5)
    d_query = jnp.einsum("hdk,hkq->hdq", keys, d_scores, preferred_element_type=F32) * scale
    d_key = jnp.einsum("hdq,hkq->hdk", queries, d_scores, preferred_element_type=F32) * scale
    d_val = jnp.einsum("hdq,hkq->hdk", d_out, probs.astype(BF16), preferred_element_type=F32)
    return d_query, d_key, d_val


def attention_forward(joined):
    _, cols, rows = joined.shape
    n = lax.axis_size("ctx")
    heads = cols // HD
    if heads % n == 0:
        mine = to_heads(joined, 0)
        pos = jnp.arange(n * rows, dtype=jnp.int32)
        out, log_total = attend(mine[0], mine[1], mine[2], pos)
        local = to_tokens(out[None], 1)[0]
        return local, (mine[0], mine[1], mine[2], out, log_total)
    split = joined.reshape(3, heads, HD, rows)
    gathered = lax.all_gather(split[1:], "ctx", axis=3, tiled=True)
    pos = lax.axis_index("ctx") * rows + jnp.arange(rows, dtype=jnp.int32)
    out, log_total = attend(split[0], gathered[0], gathered[1], pos)
    return out.reshape(cols, rows), (split[0], gathered[0], gathered[1], out, log_total)


def attention_backward(saved, d_attended):
    cols, rows = d_attended.shape
    n = lax.axis_size("ctx")
    heads = cols // HD
    if heads % n == 0:
        pos = jnp.arange(n * rows, dtype=jnp.int32)
        d_out = to_heads(d_attended[None], 1)[0]
        parts = attend_backward(*saved, d_out, pos)
        return to_tokens(jnp.stack([part.astype(BF16) for part in parts]), 0)
    pos = lax.axis_index("ctx") * rows + jnp.arange(rows, dtype=jnp.int32)
    d_query, d_key, d_val = attend_backward(*saved, d_attended.reshape(heads, HD, rows), pos)
    d_kv = lax.psum_scatter(
        jnp.stack([d_key, d_val]).astype(BF16), "ctx", scatter_dimension=3, tiled=True
    )
    return jnp.concatenate([d_query.astype(BF16)[None], d_kv]).reshape(3, cols, rows)


def layer_forward(layer_in, weights, vecs):
    w_qkv, w_out, w_fc, w_proj = weights
    b_q, b_v, b_out, b_fc, b_proj, gain_a, gain_b, shift_a, shift_b = vecs
    rows, width = layer_in.shape
    cols = w_out.shape[0]
    layer_f32 = layer_in.astype(F32)
    first, normed_a, inv_a = norm_forward(layer_f32, gain_a, shift_a)
    first = first.astype(BF16)
    joined = dot(w_qkv, first, 0, 1).reshape(3, cols, rows)
    bias = jnp.stack([b_q, jnp.zeros_like(b_q), b_v])[:, :, None]
    attended, attn_saved = attention_forward((joined + bias).astype(BF16))
    hidden = layer_f32 + tp_sum(dot(attended, w_out, 0, 0)) + b_out
    second, normed_b, inv_b = norm_forward(hidden, gain_b, shift_b)
    second = second.astype(BF16)
    act, slope = gelu_parts(dot(second, w_fc, 1, 0) + b_fc)
    act = act.astype(BF16)
    result = (hidden + tp_sum(dot(act, w_proj, 1, 0)) + b_proj).astype(BF16)
    return result, (normed_a, inv_a, first, attended, attn_saved, normed_b, inv_b, second, act, slope)


def cross(later, split, whole):
    half = split.shape[1] // 2
    low, high = split[:, :half], split[:, half:]
    sent = jnp.concatenate([jnp.where(later, low, high), whole], axis=1)
    got = swap(sent)
    both = jnp.concatenate([jnp.concatenate([jnp.where(later, high, low), whole], axis=1), got])
    return both[:, :half], both[:, half:]


def half_grad(later, split, whole):
    mine, other = cross(later, split, whole)
    return dot(mine, other, 0, 0).astype(BF16)


def ctx_sums(queue, values):
    if queue:
        values, queue[-1] = lax.optimization_barrier((values, queue[-1]))
    queue.append([lax.psum(value, "ctx") for value in values])


def layer_backward(upstream, saved, weights, vecs, later, queue):
    w_qkv, w_out, w_fc, w_proj = weights
    _, _, _, _, _, gain_a, gain_b, _, _ = vecs
    normed_a, inv_a, first, attended, attn_saved, normed_b, inv_b, second, act, slope = saved
    up_bf = upstream.astype(BF16)
    d_pre = dot(up_bf, w_proj, 1, 1) * slope
    d_pre_bf = d_pre.astype(BF16)
    d_second = tp_sum(dot(d_pre_bf, w_fc, 1, 1))
    g_proj = half_grad(later, act, up_bf)
    g_fc = half_grad(later, second, d_pre_bf)
    ctx_sums(queue, [g_proj, g_fc])
    d_hidden_ln, gain_b_grad, shift_b_grad = norm_backward(d_second, normed_b, inv_b, gain_b)
    d_hidden = upstream + d_hidden_ln
    hidden_bf = d_hidden.astype(BF16)
    d_attended = dot(w_out, hidden_bf, 1, 1).astype(BF16)
    g_out = half_grad(later, attended.T, hidden_bf)
    d_joined = attention_backward(attn_saved, d_attended)
    _, cols, rows = d_joined.shape
    flat = d_joined.reshape(3 * cols, rows)
    d_first = tp_sum(dot(flat, w_qkv, 0, 1))
    g_qkv = half_grad(later, first, flat.T)
    d_in_ln, gain_a_grad, shift_a_grad = norm_backward(d_first, normed_a, inv_a, gain_a)
    bias_grads = jnp.sum(d_joined.astype(F32), axis=2)
    small = jnp.concatenate(
        [
            bias_grads[0],
            bias_grads[2],
            jnp.sum(d_hidden, axis=0),
            jnp.sum(d_pre, axis=0),
            jnp.sum(upstream, axis=0),
            gain_a_grad,
            gain_b_grad,
            shift_a_grad,
            shift_b_grad,
        ]
    )
    return d_hidden + d_in_ln, [g_out, g_qkv], small


def body(
    layer_input, cotangent, w_qkv, b_qv, w_out, b_out, w_fc, b_fc, w_proj, b_proj, ln_gain, ln_bias
):
    later = lax.axis_index("section") == 1
    width = layer_input.shape[2]
    cols = w_out.shape[1]

    def both_layers(own):
        other = swap(own)
        return jnp.where(later, other, own), jnp.where(later, own, other)

    vec_parts = [
        b_qv[0, 0], b_qv[0, 1], b_out[0], b_fc[0], b_proj[0],
        ln_gain[0, 0], ln_gain[0, 1], ln_bias[0, 0], ln_bias[0, 1],
    ]
    bounds = []
    for part in vec_parts:
        bounds.append((bounds[-1] if bounds else 0) + part.shape[0])
    vec_pair = both_layers(jnp.concatenate([part.astype(F32) for part in vec_parts]))
    vecs = [jnp.split(vec, bounds[:-1]) for vec in vec_pair]
    mats = [
        both_layers(mat)
        for mat in (w_qkv[0].reshape(width, 3 * cols), w_out[0], w_fc[0], w_proj[0])
    ]
    weights = [[pair[layer] for pair in mats] for layer in range(2)]

    start = jnp.where(later, layer_input[1], layer_input[0])
    act_0, saved_0 = layer_forward(start, weights[0], vecs[0])
    act_1, saved_1 = layer_forward(act_0, weights[1], vecs[1])
    got_act = swap(jnp.where(later, act_0, act_1))
    activations = jnp.stack([jnp.where(later, got_act, act_0), jnp.where(later, act_1, got_act)])

    upstream = jnp.where(later, cotangent[1], cotangent[0]).astype(F32)
    queue = []
    d_1, attn_1, small_1 = layer_backward(upstream, saved_1, weights[1], vecs[1], later, queue)
    ctx_sums(queue, attn_1)
    d_0, attn_0, small_0 = layer_backward(d_1, saved_0, weights[0], vecs[0], later, queue)
    small = jnp.where(later, small_1, small_0) + swap(jnp.where(later, small_0, small_1))
    ctx_sums(queue, attn_0 + [small])
    small = queue[3].pop()
    sums_1, sums_0 = queue[0] + queue[1], queue[2] + queue[3]
    up_1 = [lax.ppermute(half, "section", [(0, 1)]) for half in sums_1]
    down_0 = [lax.ppermute(half, "section", [(1, 0)]) for half in sums_0]

    got_grad = swap(jnp.where(later, d_0, d_1).astype(BF16)).astype(F32)
    input_grads = jnp.stack([jnp.where(later, got_grad, d_0), jnp.where(later, d_1, got_grad)])

    def joined_halves(own_0, own_1, got_0, got_1):
        low = jnp.where(later, got_1, own_0)
        high = jnp.where(later, own_1, got_0)
        return jnp.concatenate([low, high]).astype(F32)

    g_proj, g_fc, g_out, g_qkv = [
        joined_halves(*group) for group in zip(sums_0, sums_1, down_0, up_1)
    ]
    small = jnp.split(small, bounds[:-1])
    return (
        activations[None],
        input_grads[None],
        g_qkv.reshape(1, width, 3, cols),
        jnp.stack([small[0], small[1]])[None],
        g_out[None],
        small[2][None],
        g_fc[None],
        small[3][None],
        g_proj[None],
        small[4][None],
        jnp.stack([small[5], small[6]])[None],
        jnp.stack([small[7], small[8]])[None],
    )


def solution(mesh):
    placed = (
        P(None, "ctx", None),
        P(None, "ctx", None),
        P("section", None, None, "tp"),
        P("section", None, "tp"),
        P("section", "tp", None),
        P("section", None),
        P("section", None, "tp"),
        P("section", "tp"),
        P("section", "tp", None),
        P("section", None),
        P("section", None, None),
        P("section", None, None),
    )
    return jax.shard_map(
        body,
        mesh=mesh,
        in_specs=placed,
        out_specs=(
            P("section", None, "ctx", None),
            P("section", None, "ctx", None),
            P("section", None, None, "tp"),
            P("section", None, "tp"),
            P("section", "tp", None),
            P("section", None),
            P("section", None, "tp"),
            P("section", "tp"),
            P("section", "tp", None),
            P("section", None),
            P("section", None, None),
            P("section", None, None),
        ),
        check_vma=False,
    )
```

time: 1670 us -> 816 us (0.49)
  waiting for transfers between devices: 1240 us -> 389 us
  matrix products: 188 us -> 78.4 us
  Pallas kernels: 0 us -> 91.2 us
  starting transfers between devices: 10.9 us -> 60.7 us
  local copies, waits for them, and re-layouts: 87.4 us -> 53.5 us
    all_gather x12 -> x0, waiting for transfers between devices: 356 us -> none  [the longest x3 105 us: layer_forward(): lax.all_gather(key_rows, 'ctx', axis=0, tiled=True)]
    unnamed x34 -> x4, waiting for transfers between devices: 336 us -> 0.07 us
    psum x10 -> x4, waiting for transfers between devices: 544 us -> 383 us  [ctx_sums(): queue.append([lax.psum(value, 'ctx') for value in values])]
    dot_general x57 -> x36, matrix products: 188 us -> 78.4 us  [the longest x24 65.2 us: dot(): lax.dot_general(lhs, rhs, (((lhs_dim,), (rhs_dim,)), ((), ())), preferred...]
    pallas_call x0 -> x8, Pallas kernels: none -> 91.2 us  [all_to_all(): pl.pallas_call(functools.partial(a2a_kernel, n), out_shape=jax.ShapeDtype...]
    ppermute x4 -> x32, starting transfers between devices: 8.53 us -> 60.6 us  [the longest x16 25 us: swap(): return lax.ppermute(value, 'section', [(0, 1), (1, 0)])]
    all_gather x12 -> x0, local copies, waits for them, and re-layouts: 26.4 us -> none  [the longest x3 6.81 us: layer_backward(): lax.all_gather(held_keys[0], 'ctx', axis=0, tiled=True)]
    concatenate x0 -> x16, other arithmetic: none -> 19.9 us  [the longest x6 8.92 us: joined_halves(): return jnp.concatenate([low, high]).astype(F32)]
  transfers between devices with their start and end apart: 32 -> 36, of which waited for: 30 -> 6; matrix products, arithmetic and copies ran while one was open for 14% -> 21% of each run, Pallas kernels for 0% -> 9%
where the time goes in v1:
time: 816 us; the launch traced here: 806 us
  waiting for transfers between devices  389 us (48%)
  Pallas kernels  91.2 us (11%)
  other arithmetic  85.9 us (11%)
  matrix products  78.4 us (10%)
  starting transfers between devices  60.7 us (7%)
  local copies, waits for them, and re-layouts  53.5 us (7%)
  blocking collectives  30.9 us (4%)
  between operations  15.9 us (2%)
    psum x4, waiting for transfers between devices, ctx_sums(): queue.append([lax.psum(value, 'ctx') for value in values])  383 us
    pallas_call x8, Pallas kernels, all_to_all(): pl.pallas_call(functools.partial(a2a_kernel, n), out_shape=jax.ShapeDtype...  91.2 us
    dot_general x24, matrix products, dot(): lax.dot_general(lhs, rhs, (((lhs_dim,), (rhs_dim,)), ((), ())), preferred...  65.2 us
    psum x1, blocking collectives, ctx_sums(): queue.append([lax.psum(value, 'ctx') for value in values])  30.9 us
    unnamed x234, local copies, waits for them, and re-layouts  27.4 us
    ppermute x16, starting transfers between devices, swap(): return lax.ppermute(value, 'section', [(0, 1), (1, 0)])  25 us
    ppermute x4, starting transfers between devices, body(): down_0 = [lax.ppermute(half, 'section', [(1, 0)]) for half in sums_0]  21.9 us
    convert_element_type x4, other arithmetic, joined_halves(): return jnp.concatenate([low, high]).astype(F32)  16.8 us
  transfers between devices with their start and end apart: 36, of which 6 were waited for; matrix products, arithmetic and copies ran while one was open for 21% of the time, Pallas kernels for 9%

profile of v1, /device:TPU:1, one launch (start us, length us, event | category | flops | bytes accessed | tf_op | source)
XLA Modules:
  0.0 805.5 jit_solution(2782005061649905782)
XLA Ops:
  7.3 3.2 copy.40
  23.5 13.3 %a2a.8 = bf16[8,192,128]{2,1,0:T(8,128)(2,1)} custom-call(bf16[8,192,128]{2,1,0:T(8,128)(2,1)} %bitcast.359), custom_call_target="tpu_custom_call" | custom-call | tf_op jit(solution)/shard_map/a2a/pallas_call | solution.py:95
  42.0 10.4 %a2a.9 = bf16[8,64,128]{2,1,0:T(8,128)(2,1)} custom-call(bf16[8,64,128]{2,1,0:T(8,128)(2,1)} %bitcast.386), custom_call_target="tpu_custom_call" | custom-call | tf_op jit(solution)/shard_map/a2a/pallas_call | solution.py:95
  65.6 5.8 multiply_convert_fusion.3
  71.4 3.3 fusion.20
  77.6 3.2 collective-permute-done.6
  84.0 12.9 %a2a.10 = bf16[8,192,128]{2,1,0:T(8,128)(2,1)} custom-call(bf16[8,192,128]{2,1,0:T(8,128)(2,1)} %bitcast.362), custom_call_target="tpu_custom_call" | custom-call | tf_op jit(solution)/shard_map/a2a/pallas_call | solution.py:95
  101.9 9.6 %a2a.11 = bf16[8,64,128]{2,1,0:T(8,128)(2,1)} custom-call(bf16[8,64,128]{2,1,0:T(8,128)(2,1)} %bitcast.387), custom_call_target="tpu_custom_call" | custom-call | tf_op jit(solution)/shard_map/a2a/pallas_call | solution.py:95
  126.1 3.5 multiply_convert_fusion.2
  138.6 11.5 %collective-permute-start.19 = (bf16[128,2048]{1,0:T(8,128)(2,1)}, bf16[128,2048]{1,0:T(8,128)(2,1)}, u32[]{:S(2)}, u32[]{:S(2)}) collective-permute-start(bf16[128,2048]{1,0:T(8,128)(2,1)} %pad_maximum_fusion.30), channel_id=1, source_target_pairs={{0,16},{16,0},{1,17},{17,1},{2,18},{18,2},{3,19},{19,3},{4,20},{20... | collective-permute-start | bytes 1572872 | tf_op jit(solution)/shard_map/ppermute | solution.py:51
  154.8 8.0 a2a.12
  171.8 9.8 %a2a.13 = bf16[8,192,128]{2,1,0:T(8,128)(2,1)} custom-call(bf16[8,192,128]{2,1,0:T(8,128)(2,1)} %bitcast.357), custom_call_target="tpu_custom_call" | custom-call | tf_op jit(solution)/shard_map/a2a/pallas_call | solution.py:95
  186.3 6.7 collective-permute-start.9
  212.6 3.2 convolution_convert_fusion
  216.0 6.2 fusion.233
  222.2 5.0 fusion.22
  245.4 10.6 %a2a.14 = bf16[8,64,128]{2,1,0:T(8,128)(2,1)} custom-call(bf16[8,64,128]{2,1,0:T(8,128)(2,1)} %bitcast.399), custom_call_target="tpu_custom_call" | custom-call | tf_op jit(solution)/shard_map/a2a/pallas_call | solution.py:95
  257.0 118.3 %all-reduce.15.cloned.1.call-done = (bf16[1024,1024]{1,0:T(8,128)(2,1)}, bf16[512,2048]{1,0:T(8,128)(2,1)}) async-done(((bf16[1024,1024]{1,0:T(8,128)(2,1)}, bf16[512,2048]{1,0:T(8,128)(2,1)}), (bf16[1024,1024]{1,0:T(8,128)(2,1)}, bf16[512,2048]{1,0:T(8,128)(2,1)})) %all-reduce.15.cloned.1.call-update) | async-done | bytes 4194320 | tf_op jit(solution)/shard_map/psum | solution.py:233
  375.4 3.2 multiply_convert_fusion
  381.5 16.7 %a2a.15 = bf16[8,192,128]{2,1,0:T(8,128)(2,1)} custom-call(bf16[8,192,128]{2,1,0:T(8,128)(2,1)} %bitcast.358), custom_call_target="tpu_custom_call" | custom-call | tf_op jit(solution)/shard_map/a2a/pallas_call | solution.py:95
  406.2 3.3 convolution_convert_fusion.1
  409.5 78.3 %all-reduce.13.cloned.1.call-done = (bf16[256,1024]{1,0:T(8,128)(2,1)}, bf16[512,1536]{1,0:T(8,128)(2,1)}) async-done(((bf16[256,1024]{1,0:T(8,128)(2,1)}, bf16[512,1536]{1,0:T(8,128)(2,1)}), (bf16[256,1024]{1,0:T(8,128)(2,1)}, bf16[512,1536]{1,0:T(8,128)(2,1)})) %all-reduce.13.cloned.1.call-update) | async-done | bytes 2097168 | tf_op jit(solution)/shard_map/psum | solution.py:233
  508.0 140.0 %all-reduce.11.cloned.1.call-done = (bf16[1024,1024]{1,0:T(8,128)(2,1)}, bf16[512,2048]{1,0:T(8,128)(2,1)}) async-done(((bf16[1024,1024]{1,0:T(8,128)(2,1)}, bf16[512,2048]{1,0:T(8,128)(2,1)}), (bf16[1024,1024]{1,0:T(8,128)(2,1)}, bf16[512,2048]{1,0:T(8,128)(2,1)})) %all-reduce.11.cloned.1.call-update) | async-done | bytes 4194320 | tf_op jit(solution)/shard_map/psum | solution.py:233
  652.8 30.9 %psum.70 = f32[9216]{0:T(1024)S(1)} all-reduce(f32[9216]{0:T(1024)S(1)} %copy-done.49), channel_id=1, replica_groups=mesh['section'=2,'ctx'=8,'tp'=2] {'ctx'}, use_global_device_ids=true, to_apply=%region_43.44 | all-reduce | flops 9216 | bytes 73728 | tf_op jit(solution)/shard_map/psum | solution.py:233
  683.7 12.8 %collective-permute-start.29 = (bf16[512,2048]{1,0:T(8,128)(2,1)}, bf16[512,2048]{1,0:T(8,128)(2,1)}, u32[]{:S(2)}, u32[]{:S(2)}) collective-permute-start(bf16[512,2048]{1,0:T(8,128)(2,1)} %get-tuple-element.35), channel_id=1, source_target_pairs={{16,0},{17,1},{18,2},{19,3},{20,4},{21,5},{22,6},{23,7},{24,8},{25... | collective-permute-start | bytes 6291464 | tf_op jit(solution)/shard_map/ppermute | solution.py:317
  705.4 3.1 select_bitcast_fusion.3
  708.5 46.3 %all-reduce.9.cloned.1.call-done = (bf16[512,1536]{1,0:T(8,128)(2,1)}, bf16[256,1024]{1,0:T(8,128)(2,1)}) async-done(((bf16[512,1536]{1,0:T(8,128)(2,1)}, bf16[256,1024]{1,0:T(8,128)(2,1)}), (bf16[512,1536]{1,0:T(8,128)(2,1)}, bf16[256,1024]{1,0:T(8,128)(2,1)})) %all-reduce.9.cloned.1.call-update) | async-done | bytes 2097168 | tf_op jit(solution)/shard_map/psum | solution.py:233
  754.8 4.3 collective-permute-start.25
  767.1 4.3 maximum_convert_fusion
  775.1 6.1 maximum_convert_fusion.1
  787.1 4.9 maximum_convert_fusion.2
  792.0 6.6 copy.65
  (468 shorter events, 184.4 us)
Async XLA Ops:
  7.2 368.1 %all-reduce.15.cloned.1.call-start = ((), (), s32[]{:S(2)}) async-start(), calls=%async_computation.3 | async-start | bytes 8388608 | tf_op jit(solution)/shard_map/psum | solution.py:233
  11.4 41.1 %collective-permute-start.2 = (bf16[512,1024]{1,0:T(8,128)(2,1)}, bf16[512,1024]{1,0:T(8,128)(2,1)}, u32[]{:S(2)}, u32[]{:S(2)}) collective-permute-start(bf16[512,1024]{1,0:T(8,128)(2,1)} %bitcast.350), channel_id=1, source_target_pairs={{0,16},{16,0},{1,17},{17,1},{2,18},{18,2},{3,19},{19,3},{4,20},{20... | collective-permute-start | bytes 3145736 | tf_op jit(solution)/shard_map/ppermute | solution.py:51
  11.4 54.1 %collective-permute-start.4 = (bf16[1024,2048]{1,0:T(8,128)(2,1)}, bf16[1024,2048]{1,0:T(8,128)(2,1)}, u32[]{:S(2)}, u32[]{:S(2)}) collective-permute-start(bf16[1024,2048]{1,0:T(8,128)(2,1)} %bitcast.426), channel_id=1, source_target_pairs={{0,16},{16,0},{1,17},{17,1},{2,18},{18,2},{3,19},{19,3},{4,20},{20... | collective-permute-start | bytes 12582920 | tf_op jit(solution)/shard_map/ppermute | solution.py:51
  11.9 59.5 %collective-permute-start.5 = (bf16[2048,1024]{1,0:T(8,128)(2,1)}, bf16[2048,1024]{1,0:T(8,128)(2,1)}, u32[]{:S(2)}, u32[]{:S(2)}) collective-permute-start(bf16[2048,1024]{1,0:T(8,128)(2,1)} %bitcast.425), channel_id=1, source_target_pairs={{0,16},{16,0},{1,17},{17,1},{2,18},{18,2},{3,19},{19,3},{4,20},{20... | collective-permute-start | bytes 12582920 | tf_op jit(solution)/shard_map/ppermute | solution.py:51
  55.1 8.1 %collective-permute-start.3 = (bf16[128,1024]{1,0:T(8,128)(2,1)}, bf16[128,1024]{1,0:T(8,128)(2,1)}, u32[]{:S(2)}, u32[]{:S(2)}) collective-permute-start(bf16[128,1024]{1,0:T(8,128)(2,1)} %convolution_convert_fusion.11), channel_id=1, source_target_pairs={{0,1},{1,0},{2,3},{3,2},{4,5},{5,4},{6,7},{7,6},{8,9},{9,8},{10,11... | collective-permute-start | bytes 786440 | tf_op jit(solution)/shard_map/ppermute | solution.py:57
  113.9 9.1 %collective-permute-start.7 = (bf16[128,1024]{1,0:T(8,128)(2,1)}, bf16[128,1024]{1,0:T(8,128)(2,1)}, u32[]{:S(2)}, u32[]{:S(2)}) collective-permute-start(bf16[128,1024]{1,0:T(8,128)(2,1)} %convolution_convert_fusion.10), channel_id=1, source_target_pairs={{0,1},{1,0},{2,3},{3,2},{4,5},{5,4},{6,7},{7,6},{8,9},{9,8},{10,11... | collective-permute-start | bytes 786440 | tf_op jit(solution)/shard_map/ppermute | solution.py:57
  132.2 51.9 %collective-permute-start.8 = (bf16[128,1024]{1,0:T(8,128)(2,1)}, bf16[128,1024]{1,0:T(8,128)(2,1)}, u32[]{:S(2)}, u32[]{:S(2)}) collective-permute-start(bf16[128,1024]{1,0:T(8,128)(2,1)} %fusion.19), channel_id=1, source_target_pairs={{0,1},{1,0},{2,3},{3,2},{4,5},{5,4},{6,7},{7,6},{8,9},{9,8},{10,11... | collective-permute-start | bytes 786440 | tf_op jit(solution)/shard_map/ppermute | solution.py:57
  136.5 14.6 %collective-permute-start.10 = (bf16[128,1024]{1,0:T(8,128)(2,1)S(1)}, bf16[128,1024]{1,0:T(8,128)(2,1)S(1)}, u32[]{:S(2)}, u32[]{:S(2)}) collective-permute-start(bf16[128,1024]{1,0:T(8,128)(2,1)S(1)} %fusion.21), channel_id=1, source_target_pairs={{0,1},{1,0},{2,3},{3,2},{4,5},{5,4},{6,7},{7,6},{8,9},{9,8},{10,11... | collective-permute-start | bytes 786440 | tf_op jit(solution)/shard_map/ppermute | solution.py:57
  138.6 68.0 %collective-permute-start.19 = (bf16[128,2048]{1,0:T(8,128)(2,1)}, bf16[128,2048]{1,0:T(8,128)(2,1)}, u32[]{:S(2)}, u32[]{:S(2)}) collective-permute-start(bf16[128,2048]{1,0:T(8,128)(2,1)} %pad_maximum_fusion.30), channel_id=1, source_target_pairs={{0,16},{16,0},{1,17},{17,1},{2,18},{18,2},{3,19},{19,3},{4,20},{20... | collective-permute-start | bytes 1572872 | tf_op jit(solution)/shard_map/ppermute | solution.py:51
  151.0 61.5 %collective-permute-start.20 = (bf16[128,2560]{1,0:T(8,128)(2,1)}, bf16[128,2560]{1,0:T(8,128)(2,1)}, u32[]{:S(2)}, u32[]{:S(2)}) collective-permute-start(bf16[128,2560]{1,0:T(8,128)(2,1)} %pad_maximum_fusion.19), channel_id=1, source_target_pairs={{0,16},{16,0},{1,17},{17,1},{2,18},{18,2},{3,19},{19,3},{4,20},{20... | collective-permute-start | bytes 1966088 | tf_op jit(solution)/shard_map/ppermute | solution.py:51
  186.3 45.8 %collective-permute-start.9 = (bf16[128,1024]{1,0:T(8,128)(2,1)}, bf16[128,1024]{1,0:T(8,128)(2,1)}, u32[]{:S(2)}, u32[]{:S(2)}) collective-permute-start(bf16[128,1024]{1,0:T(8,128)(2,1)} %get-tuple-element.84), channel_id=1, source_target_pairs={{0,16},{16,0},{1,17},{17,1},{2,18},{18,2},{3,19},{19,3},{4,20},{20... | collective-permute-start | bytes 786440 | tf_op jit(solution)/shard_map/ppermute | solution.py:51
  194.6 15.4 %collective-permute-start.11 = (bf16[128,1024]{1,0:T(8,128)(2,1)}, bf16[128,1024]{1,0:T(8,128)(2,1)S(1)}, u32[]{:S(2)}, u32[]{:S(2)}) collective-permute-start(bf16[128,1024]{1,0:T(8,128)(2,1)} %convolution_convert_fusion.9), channel_id=1, source_target_pairs={{0,1},{1,0},{2,3},{3,2},{4,5},{5,4},{6,7},{7,6},{8,9},{9,8},{10,11... | collective-permute-start | bytes 786440 | tf_op jit(solution)/shard_map/ppermute | solution.py:57
  196.7 37.8 %collective-permute-start.17 = (bf16[128,1280]{1,0:T(8,128)(2,1)}, bf16[128,1280]{1,0:T(8,128)(2,1)}, u32[]{:S(2)}, u32[]{:S(2)}) collective-permute-start(bf16[128,1280]{1,0:T(8,128)(2,1)} %pad_maximum_fusion.34), channel_id=1, source_target_pairs={{0,16},{16,0},{1,17},{17,1},{2,18},{18,2},{3,19},{19,3},{4,20},{20... | collective-permute-start | bytes 983048 | tf_op jit(solution)/shard_map/ppermute | solution.py:51
  206.6 30.1 %collective-permute-start.18 = (bf16[128,2048]{0,1:T(8,128)(2,1)}, bf16[128,2048]{0,1:T(8,128)(2,1)}, u32[]{:S(2)}, u32[]{:S(2)}) collective-permute-start(bf16[128,2048]{0,1:T(8,128)(2,1)} %pad_maximum_fusion.29), channel_id=1, source_target_pairs={{0,16},{16,0},{1,17},{17,1},{2,18},{18,2},{3,19},{19,3},{4,20},{20... | collective-permute-start | bytes 1572872 | tf_op jit(solution)/shard_map/ppermute | solution.py:51
  215.9 271.8 %all-reduce.13.cloned.1.call-start = ((), (), s32[]{:S(2)}) async-start(), calls=%async_computation.2 | async-start | bytes 4194304 | tf_op jit(solution)/shard_map/psum | solution.py:233
  227.2 12.3 %collective-permute-start.12 = (bf16[128,1024]{1,0:T(8,128)(2,1)}, bf16[128,1024]{1,0:T(8,128)(2,1)}, u32[]{:S(2)}, u32[]{:S(2)}) collective-permute-start(bf16[128,1024]{1,0:T(8,128)(2,1)} %fusion.22), channel_id=1, source_target_pairs={{0,1},{1,0},{2,3},{3,2},{4,5},{5,4},{6,7},{7,6},{8,9},{9,8},{10,11... | collective-permute-start | bytes 786440 | tf_op jit(solution)/shard_map/ppermute | solution.py:57
  228.9 174.0 %collective-permute-start.15 = (bf16[128,2048]{1,0:T(8,128)(2,1)}, bf16[128,2048]{1,0:T(8,128)(2,1)}, u32[]{:S(2)}, u32[]{:S(2)}) collective-permute-start(bf16[128,2048]{1,0:T(8,128)(2,1)} %pad_maximum_fusion.28), channel_id=1, source_target_pairs={{0,16},{16,0},{1,17},{17,1},{2,18},{18,2},{3,19},{19,3},{4,20},{20... | collective-permute-start | bytes 1572872 | tf_op jit(solution)/shard_map/ppermute | solution.py:51
  232.1 174.0 %collective-permute-start.16 = (bf16[128,2560]{1,0:T(8,128)(2,1)}, bf16[128,2560]{1,0:T(8,128)(2,1)}, u32[]{:S(2)}, u32[]{:S(2)}) collective-permute-start(bf16[128,2560]{1,0:T(8,128)(2,1)} %pad_maximum_fusion.18), channel_id=1, source_target_pairs={{0,16},{16,0},{1,17},{17,1},{2,18},{18,2},{3,19},{19,3},{4,20},{20... | collective-permute-start | bytes 1966088 | tf_op jit(solution)/shard_map/ppermute | solution.py:51
  375.4 272.7 %all-reduce.11.cloned.1.call-start = ((), (), s32[]{:S(2)}) async-start(), calls=%async_computation.1 | async-start | bytes 8388608 | tf_op jit(solution)/shard_map/psum | solution.py:233
  401.8 88.3 %collective-permute-start.13 = (bf16[128,1024]{1,0:T(8,128)(2,1)S(1)}, bf16[128,1024]{1,0:T(8,128)(2,1)S(1)}, u32[]{:S(2)}, u32[]{:S(2)}) collective-permute-start(bf16[128,1024]{1,0:T(8,128)(2,1)S(1)} %convolution_convert_fusion.8), channel_id=1, source_target_pairs={{0,1},{1,0},{2,3},{3,2},{4,5},{5,4},{6,7},{7,6},{8,9},{9,8},{10,11... | collective-permute-start | bytes 786440 | tf_op jit(solution)/shard_map/ppermute | solution.py:57
  487.8 267.1 %all-reduce.9.cloned.1.call-start = ((), (), s32[]{:S(2)}) async-start(), calls=%async_computation | async-start | bytes 4194304 | tf_op jit(solution)/shard_map/psum | solution.py:233
  488.6 14.3 %collective-permute-start.22 = (bf16[128,1280]{1,0:T(8,128)(2,1)}, bf16[128,1280]{1,0:T(8,128)(2,1)}, u32[]{:S(2)}, u32[]{:S(2)}) collective-permute-start(bf16[128,1280]{1,0:T(8,128)(2,1)} %pad_maximum_fusion.35), channel_id=1, source_target_pairs={{0,16},{16,0},{1,17},{17,1},{2,18},{18,2},{3,19},{19,3},{4,20},{20... | collective-permute-start | bytes 983048 | tf_op jit(solution)/shard_map/ppermute | solution.py:51
  491.6 156.4 %collective-permute-start.14 = (bf16[128,1024]{1,0:T(8,128)(2,1)}, bf16[128,1024]{1,0:T(8,128)(2,1)}, u32[]{:S(2)}, u32[]{:S(2)}) collective-permute-start(bf16[128,1024]{1,0:T(8,128)(2,1)} %get-tuple-element.82), channel_id=1, source_target_pairs={{0,16},{16,0},{1,17},{17,1},{2,18},{18,2},{3,19},{19,3},{4,20},{20... | collective-permute-start | bytes 786440 | tf_op jit(solution)/shard_map/ppermute | solution.py:51
  494.2 205.3 %collective-permute-start.30 = (bf16[1024,1024]{1,0:T(8,128)(2,1)}, bf16[1024,1024]{1,0:T(8,128)(2,1)S(1)}, u32[]{:S(2)}, u32[]{:S(2)}) collective-permute-start(bf16[1024,1024]{1,0:T(8,128)(2,1)} %get-tuple-element.36), channel_id=1, source_target_pairs={{0,16},{1,17},{2,18},{3,19},{4,20},{5,21},{6,22},{7,23},{8,24},{9,... | collective-permute-start | bytes 6291464 | tf_op jit(solution)/shard_map/ppermute | solution.py:316
  497.3 7.9 collective-permute-start.23
  500.2 205.2 %collective-permute-start.28 = (bf16[512,2048]{1,0:T(8,128)(2,1)}, bf16[512,2048]{1,0:T(8,128)(2,1)}, u32[]{:S(2)}, u32[]{:S(2)}) collective-permute-start(bf16[512,2048]{1,0:T(8,128)(2,1)} %get-tuple-element.34), channel_id=1, source_target_pairs={{0,16},{1,17},{2,18},{3,19},{4,20},{5,21},{6,22},{7,23},{8,24},{9,... | collective-permute-start | bytes 6291464 | tf_op jit(solution)/shard_map/ppermute | solution.py:316
  650.2 108.9 %collective-permute-start.21 = (bf16[512,1536]{1,0:T(8,128)(2,1)}, bf16[512,1536]{1,0:T(8,128)(2,1)}, u32[]{:S(2)}, u32[]{:S(2)}) collective-permute-start(bf16[512,1536]{1,0:T(8,128)(2,1)} %get-tuple-element.27), channel_id=1, source_target_pairs={{0,16},{1,17},{2,18},{3,19},{4,20},{5,21},{6,22},{7,23},{8,24},{9,... | collective-permute-start | bytes 4718600 | tf_op jit(solution)/shard_map/ppermute | solution.py:316
  651.5 119.9 %collective-permute-start.26 = (bf16[256,1024]{1,0:T(8,128)(2,1)}, bf16[256,1024]{1,0:T(8,128)(2,1)}, u32[]{:S(2)}, u32[]{:S(2)}) collective-permute-start(bf16[256,1024]{1,0:T(8,128)(2,1)} %get-tuple-element.32), channel_id=1, source_target_pairs={{0,16},{1,17},{2,18},{3,19},{4,20},{5,21},{6,22},{7,23},{8,24},{9,... | collective-permute-start | bytes 1572872 | tf_op jit(solution)/shard_map/ppermute | solution.py:316
  683.7 80.3 %collective-permute-start.29 = (bf16[512,2048]{1,0:T(8,128)(2,1)}, bf16[512,2048]{1,0:T(8,128)(2,1)}, u32[]{:S(2)}, u32[]{:S(2)}) collective-permute-start(bf16[512,2048]{1,0:T(8,128)(2,1)} %get-tuple-element.35), channel_id=1, source_target_pairs={{16,0},{17,1},{18,2},{19,3},{20,4},{21,5},{22,6},{23,7},{24,8},{25... | collective-permute-start | bytes 6291464 | tf_op jit(solution)/shard_map/ppermute | solution.py:317
  700.9 63.3 %collective-permute-start.31 = (bf16[1024,1024]{1,0:T(8,128)(2,1)}, bf16[1024,1024]{1,0:T(8,128)(2,1)}, u32[]{:S(2)}, u32[]{:S(2)}) collective-permute-start(bf16[1024,1024]{1,0:T(8,128)(2,1)} %get-tuple-element.37), channel_id=1, source_target_pairs={{16,0},{17,1},{18,2},{19,3},{20,4},{21,5},{22,6},{23,7},{24,8},{25... | collective-permute-start | bytes 6291464 | tf_op jit(solution)/shard_map/ppermute | solution.py:317
  754.8 29.0 %collective-permute-start.25 = (bf16[512,1536]{1,0:T(8,128)(2,1)}, bf16[512,1536]{1,0:T(8,128)(2,1)}, u32[]{:S(2)}, u32[]{:S(2)}) collective-permute-start(bf16[512,1536]{1,0:T(8,128)(2,1)} %get-tuple-element.66), channel_id=1, source_target_pairs={{16,0},{17,1},{18,2},{19,3},{20,4},{21,5},{22,6},{23,7},{24,8},{25... | collective-permute-start | bytes 4718600 | tf_op jit(solution)/shard_map/ppermute | solution.py:317
  759.1 22.0 %collective-permute-start.27 = (bf16[256,1024]{1,0:T(8,128)(2,1)}, bf16[256,1024]{1,0:T(8,128)(2,1)}, u32[]{:S(2)}, u32[]{:S(2)}) collective-permute-start(bf16[256,1024]{1,0:T(8,128)(2,1)} %get-tuple-element.67), channel_id=1, source_target_pairs={{16,0},{17,1},{18,2},{19,3},{20,4},{21,5},{22,6},{23,7},{24,8},{25... | collective-permute-start | bytes 1572872 | tf_op jit(solution)/shard_map/ppermute | solution.py:317
  (104 other events, 1968.5 us)
Sparse Core Ops, SparseCore 0:
  216.0 159.2 all-reduce.14
  379.1 108.6 all-reduce.12
  492.0 155.9 all-reduce.10
  652.7 102.1 all-reduce.8

commit v2 on v1

--- a/solution.py
+++ b/solution.py
@@ -224,16 +224,50 @@
 
 def half_grad(later, split, whole):
     mine, other = cross(later, split, whole)
-    return dot(mine, other, 0, 0).astype(BF16)
-
-
-def ctx_sums(queue, values):
-    if queue:
-        values, queue[-1] = lax.optimization_barrier((values, queue[-1]))
-    queue.append([lax.psum(value, "ctx") for value in values])
-
-
-def layer_backward(upstream, saved, weights, vecs, later, queue):
+    return dot(mine, other, 0, 0)
+
+
+def tree_sum(value, order):
+    n = lax.axis_size("ctx")
+    me = lax.axis_index("ctx")
+
+    def partner(part, bit):
+        return lax.ppermute(part, "ctx", [(source, source ^ bit) for source in range(n)])
+
+    for bit in order:
+        upper = lax.rem(me // bit, 2) == 1
+        half = value.shape[0] // 2
+        low, high = value[:half], value[half:]
+        got = partner(jnp.where(upper, low, high).astype(BF16), bit)
+        value = jnp.where(upper, high, low) + got.astype(F32)
+    value = value.astype(BF16)
+    for bit in order[::-1]:
+        upper = lax.rem(me // bit, 2) == 1
+        got = partner(value, bit)
+        value = jnp.where(
+            upper, jnp.concatenate([got, value]), jnp.concatenate([value, got])
+        )
+    return value
+
+
+def attn_sums(g_out, g_qkv):
+    n = lax.axis_size("ctx")
+    rows, width = g_qkv.shape
+    fold = rows // g_out.shape[0]
+    if n & (n - 1) or rows % (2 * n) or rows % g_out.shape[0] or g_out.shape[1] % fold:
+        return [lax.psum(g_out.astype(BF16), "ctx"), lax.psum(g_qkv.astype(BF16), "ctx")]
+    bits = [1 << power for power in range(n.bit_length() - 1)]
+    folded = jnp.concatenate(jnp.split(g_out, fold, axis=1), axis=0)
+    both = jnp.concatenate([g_qkv, folded], axis=1)
+    half = rows // 2
+    total = jnp.concatenate(
+        [tree_sum(both[:half], bits), tree_sum(both[half:], bits[1:] + bits[:1])]
+    )
+    out = jnp.concatenate(jnp.split(total[:, width:], fold, axis=0), axis=1)
+    return [out, total[:, :width]]
+
+
+def layer_backward(upstream, saved, weights, vecs, later):
     w_qkv, w_out, w_fc, w_proj = weights
     _, _, _, _, _, gain_a, gain_b, _, _ = vecs
     normed_a, inv_a, first, attended, attn_saved, normed_b, inv_b, second, act, slope = saved
@@ -241,9 +275,8 @@
     d_pre = dot(up_bf, w_proj, 1, 1) * slope
     d_pre_bf = d_pre.astype(BF16)
     d_second = tp_sum(dot(d_pre_bf, w_fc, 1, 1))
-    g_proj = half_grad(later, act, up_bf)
-    g_fc = half_grad(later, second, d_pre_bf)
-    ctx_sums(queue, [g_proj, g_fc])
+    g_proj = half_grad(later, act, up_bf).astype(BF16)
+    g_fc = half_grad(later, second, d_pre_bf).astype(BF16)
     d_hidden_ln, gain_b_grad, shift_b_grad = norm_backward(d_second, normed_b, inv_b, gain_b)
     d_hidden = upstream + d_hidden_ln
     hidden_bf = d_hidden.astype(BF16)
@@ -269,7 +302,7 @@
             shift_b_grad,
         ]
     )
-    return d_hidden + d_in_ln, [g_out, g_qkv], small
+    return d_hidden + d_in_ln, (g_proj, g_fc), (g_out, g_qkv), small
 
 
 def body(
@@ -305,14 +338,23 @@
     activations = jnp.stack([jnp.where(later, got_act, act_0), jnp.where(later, act_1, got_act)])
 
     upstream = jnp.where(later, cotangent[1], cotangent[0]).astype(F32)
-    queue = []
-    d_1, attn_1, small_1 = layer_backward(upstream, saved_1, weights[1], vecs[1], later, queue)
-    ctx_sums(queue, attn_1)
-    d_0, attn_0, small_0 = layer_backward(d_1, saved_0, weights[0], vecs[0], later, queue)
+    d_1, ffn_1, attn_1, small_1 = layer_backward(upstream, saved_1, weights[1], vecs[1], later)
+    ffn_1 = [lax.psum(half, "ctx") for half in ffn_1]
+    attn_1 = attn_sums(*attn_1)
+    d_0, ffn_0, attn_0, small_0 = layer_backward(d_1, saved_0, weights[0], vecs[0], later)
     small = jnp.where(later, small_1, small_0) + swap(jnp.where(later, small_0, small_1))
-    ctx_sums(queue, attn_0 + [small])
-    small = queue[3].pop()
-    sums_1, sums_0 = queue[0] + queue[1], queue[2] + queue[3]
+    g_proj_0, g_fc_0 = ffn_0
+    span = g_fc_0.shape[1]
+    small_rows = -(-small.shape[0] // span)
+    small_rows += -small_rows % 16
+    small_pad = jnp.pad(small.astype(BF16), (0, small_rows * span - small.shape[0]))
+    last = [g_proj_0, jnp.concatenate([g_fc_0, small_pad.reshape(small_rows, span)])]
+    last, ffn_1, attn_0 = lax.optimization_barrier((last, ffn_1, attn_0))
+    attn_0 = attn_sums(*attn_0)
+    g_proj_0, packed = [lax.psum(half, "ctx") for half in last]
+    small = packed[-small_rows:].astype(F32).reshape(-1)[: small.shape[0]]
+    sums_1 = ffn_1 + attn_1
+    sums_0 = [g_proj_0, packed[:-small_rows]] + attn_0
     up_1 = [lax.ppermute(half, "section", [(0, 1)]) for half in sums_1]
     down_0 = [lax.ppermute(half, "section", [(1, 0)]) for half in sums_0]
 

time: 816 us -> 713 us (0.87)
  waiting for transfers between devices: 389 us -> 243 us
  blocking collectives: 30.9 us -> 0 us
  starting transfers between devices: 60.7 us -> 86.9 us
  other arithmetic: 85.9 us -> 110 us
  Pallas kernels: 91.2 us -> 115 us
  matrix products: 78.4 us -> 67.3 us
  local copies, waits for them, and re-layouts: 53.5 us -> 63.3 us
    psum x4 -> x2, waiting for transfers between devices: 383 us -> 69.3 us  [the longest x1 69.3 us: body(): g_proj_0, packed = [lax.psum(half, 'ctx') for half in last]]
    ppermute x0 -> x24, waiting for transfers between devices: none -> 168 us  [partner(): lax.ppermute(part, 'ctx', [(source, source ^ bit) for source in range(n)])]
    ppermute x0 -> x24, starting transfers between devices: none -> 37.5 us  [partner(): lax.ppermute(part, 'ctx', [(source, source ^ bit) for source in range(n)])]
    psum x1 -> x0, blocking collectives: 30.9 us -> none  [ctx_sums(): queue.append([lax.psum(value, 'ctx') for value in values])]
    pallas_call x8, Pallas kernels: 91.2 us -> 115 us  [all_to_all(): pl.pallas_call(functools.partial(a2a_kernel, n), out_shape=jax.ShapeDtype...]
    ppermute x4, starting transfers between devices: 21.9 us -> 9.65 us  [body(): down_0 = [lax.ppermute(half, 'section', [(1, 0)]) for half in sums_0]]
    dot_general x24, matrix products: 65.2 us -> 54.7 us  [dot(): lax.dot_general(lhs, rhs, (((lhs_dim,), (rhs_dim,)), ((), ())), preferred...]
    select_n x0 -> x12, other arithmetic: none -> 10.5 us  [tree_sum(): jnp.where(upper, jnp.concatenate([got, value]), jnp.concatenate([value, g...]
  transfers between devices with their start and end apart: 36 -> 58, of which waited for: 6 -> 20; matrix products, arithmetic and copies ran while one was open for 21% -> 28% of each run, Pallas kernels for 9% -> 13%
where the time goes in v2:
time: 713 us; the launch traced here: 703 us
  waiting for transfers between devices  243 us (34%)
  Pallas kernels  115 us (16%)
  other arithmetic  110 us (15%)
  starting transfers between devices  86.9 us (12%)
  matrix products  67.3 us (9%)
  local copies, waits for them, and re-layouts  63.3 us (9%)
  between operations  16.7 us (2%)
    ppermute x24, waiting for transfers between devices, partner(): lax.ppermute(part, 'ctx', [(source, source ^ bit) for source in range(n)])  168 us
    pallas_call x8, Pallas kernels, all_to_all(): pl.pallas_call(functools.partial(a2a_kernel, n), out_shape=jax.ShapeDtype...  115 us
    psum x1, waiting for transfers between devices, body(): g_proj_0, packed = [lax.psum(half, 'ctx') for half in last]  69.3 us
    dot_general x24, matrix products, dot(): lax.dot_general(lhs, rhs, (((lhs_dim,), (rhs_dim,)), ((), ())), preferred...  54.7 us
    ppermute x24, starting transfers between devices, partner(): lax.ppermute(part, 'ctx', [(source, source ^ bit) for source in range(n)])  37.5 us
    unnamed x269, local copies, waits for them, and re-layouts  36.4 us
    ppermute x16, starting transfers between devices, swap(): return lax.ppermute(value, 'section', [(0, 1), (1, 0)])  25.9 us
    convert_element_type x4, other arithmetic, joined_halves(): return jnp.concatenate([low, high]).astype(F32)  15.7 us
  transfers between devices with their start and end apart: 58, of which 20 were waited for; matrix products, arithmetic and copies ran while one was open for 28% of the time, Pallas kernels for 13%

profile of v2, /device:TPU:1, one launch (start us, length us, event | category | flops | bytes accessed | tf_op | source)
XLA Modules:
  0.0 702.5 jit_solution(2698571255866162949)
XLA Ops:
  23.6 13.2 %a2a.8 = bf16[8,192,128]{2,1,0:T(8,128)(2,1)} custom-call(bf16[8,192,128]{2,1,0:T(8,128)(2,1)} %bitcast.361), custom_call_target="tpu_custom_call" | custom-call | tf_op jit(solution)/shard_map/a2a/pallas_call | solution.py:95
  42.3 10.4 %a2a.9 = bf16[8,64,128]{2,1,0:T(8,128)(2,1)} custom-call(bf16[8,64,128]{2,1,0:T(8,128)(2,1)} %bitcast.388), custom_call_target="tpu_custom_call" | custom-call | tf_op jit(solution)/shard_map/a2a/pallas_call | solution.py:95
  65.9 5.8 multiply_convert_fusion.3
  84.4 12.8 %a2a.10 = bf16[8,192,128]{2,1,0:T(8,128)(2,1)} custom-call(bf16[8,192,128]{2,1,0:T(8,128)(2,1)} %bitcast.364), custom_call_target="tpu_custom_call" | custom-call | tf_op jit(solution)/shard_map/a2a/pallas_call | solution.py:95
  102.7 9.6 %a2a.11 = bf16[8,64,128]{2,1,0:T(8,128)(2,1)} custom-call(bf16[8,64,128]{2,1,0:T(8,128)(2,1)} %bitcast.389), custom_call_target="tpu_custom_call" | custom-call | tf_op jit(solution)/shard_map/a2a/pallas_call | solution.py:95
  139.5 11.5 %collective-permute-start.33 = (bf16[128,2048]{1,0:T(8,128)(2,1)}, bf16[128,2048]{1,0:T(8,128)(2,1)}, u32[]{:S(2)}, u32[]{:S(2)}) collective-permute-start(bf16[128,2048]{1,0:T(8,128)(2,1)} %pad_maximum_fusion.33), channel_id=1, source_target_pairs={{0,16},{16,0},{1,17},{17,1},{2,18},{18,2},{3,19},{19,3},{4,20},{20... | collective-permute-start | bytes 1572872 | tf_op jit(solution)/shard_map/ppermute | solution.py:51
  155.6 8.0 %a2a.12 = bf16[8,64,128]{2,1,0:T(8,128)(2,1)} custom-call(bf16[8,64,128]{2,1,0:T(8,128)(2,1)} %bitcast.404), custom_call_target="tpu_custom_call" | custom-call | tf_op jit(solution)/shard_map/a2a/pallas_call | solution.py:95
  172.3 9.8 %a2a.13 = bf16[8,192,128]{2,1,0:T(8,128)(2,1)} custom-call(bf16[8,192,128]{2,1,0:T(8,128)(2,1)} %bitcast.359), custom_call_target="tpu_custom_call" | custom-call | tf_op jit(solution)/shard_map/a2a/pallas_call | solution.py:95
  186.8 6.8 collective-permute-start.9
  214.1 5.0 fusion.239
  219.1 4.6 fusion.22
  247.6 32.1 %a2a.14 = bf16[8,64,128]{2,1,0:T(8,128)(2,1)} custom-call(bf16[8,64,128]{2,1,0:T(8,128)(2,1)} %bitcast.403), custom_call_target="tpu_custom_call" | custom-call | tf_op jit(solution)/shard_map/a2a/pallas_call | solution.py:95
  287.4 18.6 %a2a.15 = bf16[8,192,128]{2,1,0:T(8,128)(2,1)} custom-call(bf16[8,192,128]{2,1,0:T(8,128)(2,1)} %bitcast.360), custom_call_target="tpu_custom_call" | custom-call | tf_op jit(solution)/shard_map/a2a/pallas_call | solution.py:95
  338.2 20.5 %collective-permute-done.24 = bf16[64,2048]{1,0:T(8,128)(2,1)S(1)} collective-permute-done((bf16[64,2048]{1,0:T(8,128)(2,1)S(1)}, bf16[64,2048]{1,0:T(8,128)(2,1)S(1)}, u32[]{:S(2)}, u32[]{:S(2)}) %collective-permute-start.24) | collective-permute-done | bytes 262176 | tf_op jit(solution)/shard_map/ppermute | solution.py:235
  364.7 5.3 collective-permute-done.19
  374.5 9.5 %collective-permute-done.20 = bf16[32,2048]{1,0:T(8,128)(2,1)S(1)} collective-permute-done((bf16[32,2048]{1,0:T(8,128)(2,1)S(1)}, bf16[32,2048]{1,0:T(8,128)(2,1)S(1)}, u32[]{:S(2)}, u32[]{:S(2)}) %collective-permute-start.20) | collective-permute-done | bytes 131104 | tf_op jit(solution)/shard_map/ppermute | solution.py:235
  384.7 12.4 %collective-permute-start.21 = (bf16[64,2048]{1,0:T(8,128)(2,1)}, bf16[64,2048]{1,0:T(8,128)(2,1)}, u32[]{:S(2)}, u32[]{:S(2)}) collective-permute-start(bf16[64,2048]{1,0:T(8,128)(2,1)} %maximum_select_fusion.8), channel_id=1, source_target_pairs={{0,4},{2,6},{4,0},{6,2},{8,12},{10,14},{12,8},{14,10},{1,5},{3,7},... | collective-permute-start | bytes 786440 | tf_op jit(solution)/shard_map/ppermute | solution.py:235
  397.2 13.3 %collective-permute-done.27 = bf16[64,2048]{1,0:T(8,128)(2,1)S(1)} collective-permute-done((bf16[64,2048]{1,0:T(8,128)(2,1)S(1)}, bf16[64,2048]{1,0:T(8,128)(2,1)S(1)}, u32[]{:S(2)}, u32[]{:S(2)}) %collective-permute-start.27) | collective-permute-done | bytes 262176 | tf_op jit(solution)/shard_map/ppermute | solution.py:235
  417.2 10.8 %collective-permute-done.21 = bf16[64,2048]{1,0:T(8,128)(2,1)} collective-permute-done((bf16[64,2048]{1,0:T(8,128)(2,1)}, bf16[64,2048]{1,0:T(8,128)(2,1)}, u32[]{:S(2)}, u32[]{:S(2)}) %collective-permute-start.21) | collective-permute-done | bytes 262176 | tf_op jit(solution)/shard_map/ppermute | solution.py:235
  430.2 9.5 %collective-permute-done.28 = bf16[128,2048]{1,0:T(8,128)(2,1)} collective-permute-done((bf16[128,2048]{1,0:T(8,128)(2,1)}, bf16[128,2048]{1,0:T(8,128)(2,1)}, u32[]{:S(2)}, u32[]{:S(2)}) %collective-permute-start.28) | collective-permute-done | bytes 524320 | tf_op jit(solution)/shard_map/ppermute | solution.py:235
  450.9 7.6 %collective-permute-done.37 = bf16[128,2048]{1,0:T(8,128)(2,1)} collective-permute-done((bf16[128,2048]{1,0:T(8,128)(2,1)}, bf16[128,2048]{1,0:T(8,128)(2,1)}, u32[]{:S(2)}, u32[]{:S(2)}) %collective-permute-start.37) | collective-permute-done | bytes 524320 | tf_op jit(solution)/shard_map/ppermute | solution.py:235
  466.3 22.7 %collective-permute-done.44 = bf16[64,2048]{1,0:T(8,128)(2,1)S(1)} collective-permute-done((bf16[64,2048]{1,0:T(8,128)(2,1)S(1)}, bf16[64,2048]{1,0:T(8,128)(2,1)S(1)}, u32[]{:S(2)}, u32[]{:S(2)}) %collective-permute-start.44) | collective-permute-done | bytes 262176 | tf_op jit(solution)/shard_map/ppermute | solution.py:235
  494.8 13.0 %collective-permute-done.39 = bf16[32,2048]{1,0:T(8,128)(2,1)S(1)} collective-permute-done((bf16[32,2048]{1,0:T(8,128)(2,1)S(1)}, bf16[32,2048]{1,0:T(8,128)(2,1)S(1)}, u32[]{:S(2)}, u32[]{:S(2)}) %collective-permute-start.39) | collective-permute-done | bytes 131104 | tf_op jit(solution)/shard_map/ppermute | solution.py:235
  510.4 20.8 %collective-permute-done.40 = bf16[32,2048]{1,0:T(8,128)(2,1)S(1)} collective-permute-done((bf16[32,2048]{1,0:T(8,128)(2,1)S(1)}, bf16[32,2048]{1,0:T(8,128)(2,1)S(1)}, u32[]{:S(2)}, u32[]{:S(2)}) %collective-permute-start.40) | collective-permute-done | bytes 131104 | tf_op jit(solution)/shard_map/ppermute | solution.py:235
  531.4 10.2 %collective-permute-done.47 = bf16[64,2048]{1,0:T(8,128)(2,1)S(1)} collective-permute-done((bf16[64,2048]{1,0:T(8,128)(2,1)S(1)}, bf16[64,2048]{1,0:T(8,128)(2,1)S(1)}, u32[]{:S(2)}, u32[]{:S(2)}) %collective-permute-start.47) | collective-permute-done | bytes 262176 | tf_op jit(solution)/shard_map/ppermute | solution.py:235
  541.8 5.4 collective-permute-done.41
  553.2 11.4 %collective-permute-done.48 = bf16[128,2048]{1,0:T(8,128)(2,1)S(1)} collective-permute-done((bf16[128,2048]{1,0:T(8,128)(2,1)S(1)}, bf16[128,2048]{1,0:T(8,128)(2,1)S(1)}, u32[]{:S(2)}, u32[]{:S(2)}) %collective-permute-start.48) | collective-permute-done | bytes 524320 | tf_op jit(solution)/shard_map/ppermute | solution.py:235
  582.9 69.3 %all-reduce.6.cloned.1.call-done = (bf16[528,2048]{1,0:T(8,128)(2,1)}, bf16[1024,1024]{1,0:T(8,128)(2,1)}) async-done(((bf16[528,2048]{1,0:T(8,128)(2,1)}, bf16[1024,1024]{1,0:T(8,128)(2,1)}), (bf16[528,2048]{1,0:T(8,128)(2,1)}, bf16[1024,1024]{1,0:T(8,128)(2,1)})) %all-reduce.6.cloned.1.call-update) | async-done | bytes 4259856 | tf_op jit(solution)/shard_map/psum | solution.py:354
  663.6 5.4 maximum_convert_fusion.2
  669.0 6.6 copy.65
  684.7 4.3 maximum_convert_fusion
  690.7 4.5 maximum_convert_fusion.1
  (590 shorter events, 274.9 us)
Async XLA Ops:
  7.2 435.4 %all-reduce.8.cloned.1.call-start = ((), (), s32[]{:S(2)}) async-start(), calls=%async_computation.1 | async-start | bytes 8388608 | tf_op jit(solution)/shard_map/psum | solution.py:342
  11.4 41.4 %collective-permute-start.2 = (bf16[512,1024]{1,0:T(8,128)(2,1)}, bf16[512,1024]{1,0:T(8,128)(2,1)}, u32[]{:S(2)}, u32[]{:S(2)}) collective-permute-start(bf16[512,1024]{1,0:T(8,128)(2,1)} %bitcast.352), channel_id=1, source_target_pairs={{0,16},{16,0},{1,17},{17,1},{2,18},{18,2},{3,19},{19,3},{4,20},{20... | collective-permute-start | bytes 3145736 | tf_op jit(solution)/shard_map/ppermute | solution.py:51
  11.4 54.4 %collective-permute-start.4 = (bf16[1024,2048]{1,0:T(8,128)(2,1)}, bf16[1024,2048]{1,0:T(8,128)(2,1)}, u32[]{:S(2)}, u32[]{:S(2)}) collective-permute-start(bf16[1024,2048]{1,0:T(8,128)(2,1)} %bitcast.429), channel_id=1, source_target_pairs={{0,16},{16,0},{1,17},{17,1},{2,18},{18,2},{3,19},{19,3},{4,20},{20... | collective-permute-start | bytes 12582920 | tf_op jit(solution)/shard_map/ppermute | solution.py:51
  11.9 59.8 %collective-permute-start.5 = (bf16[2048,1024]{1,0:T(8,128)(2,1)}, bf16[2048,1024]{1,0:T(8,128)(2,1)}, u32[]{:S(2)}, u32[]{:S(2)}) collective-permute-start(bf16[2048,1024]{1,0:T(8,128)(2,1)} %bitcast.428), channel_id=1, source_target_pairs={{0,16},{16,0},{1,17},{17,1},{2,18},{18,2},{3,19},{19,3},{4,20},{20... | collective-permute-start | bytes 12582920 | tf_op jit(solution)/shard_map/ppermute | solution.py:51
  133.0 51.5 %collective-permute-start.8 = (bf16[128,1024]{1,0:T(8,128)(2,1)}, bf16[128,1024]{1,0:T(8,128)(2,1)}, u32[]{:S(2)}, u32[]{:S(2)}) collective-permute-start(bf16[128,1024]{1,0:T(8,128)(2,1)} %fusion.19), channel_id=1, source_target_pairs={{0,1},{1,0},{2,3},{3,2},{4,5},{5,4},{6,7},{7,6},{8,9},{9,8},{10,11... | collective-permute-start | bytes 786440 | tf_op jit(solution)/shard_map/ppermute | solution.py:57
  139.5 67.6 %collective-permute-start.33 = (bf16[128,2048]{1,0:T(8,128)(2,1)}, bf16[128,2048]{1,0:T(8,128)(2,1)}, u32[]{:S(2)}, u32[]{:S(2)}) collective-permute-start(bf16[128,2048]{1,0:T(8,128)(2,1)} %pad_maximum_fusion.33), channel_id=1, source_target_pairs={{0,16},{16,0},{1,17},{17,1},{2,18},{18,2},{3,19},{19,3},{4,20},{20... | collective-permute-start | bytes 1572872 | tf_op jit(solution)/shard_map/ppermute | solution.py:51
  151.9 78.9 %collective-permute-start.34 = (bf16[128,2560]{1,0:T(8,128)(2,1)}, bf16[128,2560]{1,0:T(8,128)(2,1)}, u32[]{:S(2)}, u32[]{:S(2)}) collective-permute-start(bf16[128,2560]{1,0:T(8,128)(2,1)} %pad_maximum_fusion.22), channel_id=1, source_target_pairs={{0,16},{16,0},{1,17},{17,1},{2,18},{18,2},{3,19},{19,3},{4,20},{20... | collective-permute-start | bytes 1966088 | tf_op jit(solution)/shard_map/ppermute | solution.py:51
  186.8 41.3 %collective-permute-start.9 = (bf16[128,1024]{1,0:T(8,128)(2,1)}, bf16[128,1024]{1,0:T(8,128)(2,1)}, u32[]{:S(2)}, u32[]{:S(2)}) collective-permute-start(bf16[128,1024]{1,0:T(8,128)(2,1)} %get-tuple-element.68), channel_id=1, source_target_pairs={{0,16},{16,0},{1,17},{17,1},{2,18},{18,2},{3,19},{19,3},{4,20},{20... | collective-permute-start | bytes 786440 | tf_op jit(solution)/shard_map/ppermute | solution.py:51
  197.0 32.8 %collective-permute-start.16 = (bf16[128,1280]{1,0:T(8,128)(2,1)}, bf16[128,1280]{1,0:T(8,128)(2,1)S(1)}, u32[]{:S(2)}, u32[]{:S(2)}) collective-permute-start(bf16[128,1280]{1,0:T(8,128)(2,1)} %pad_maximum_fusion.39), channel_id=1, source_target_pairs={{0,16},{16,0},{1,17},{17,1},{2,18},{18,2},{3,19},{19,3},{4,20},{20... | collective-permute-start | bytes 983048 | tf_op jit(solution)/shard_map/ppermute | solution.py:51
  207.0 27.0 %collective-permute-start.15 = (bf16[128,2048]{0,1:T(8,128)(2,1)}, bf16[128,2048]{0,1:T(8,128)(2,1)S(1)}, u32[]{:S(2)}, u32[]{:S(2)}) collective-permute-start(bf16[128,2048]{0,1:T(8,128)(2,1)} %pad_maximum_fusion.31), channel_id=1, source_target_pairs={{0,16},{16,0},{1,17},{17,1},{2,18},{18,2},{3,19},{19,3},{4,20},{20... | collective-permute-start | bytes 1572872 | tf_op jit(solution)/shard_map/ppermute | solution.py:51
  228.1 91.5 %collective-permute-start.30 = (bf16[128,2048]{1,0:T(8,128)(2,1)}, bf16[128,2048]{1,0:T(8,128)(2,1)}, u32[]{:S(2)}, u32[]{:S(2)}) collective-permute-start(bf16[128,2048]{1,0:T(8,128)(2,1)} %pad_maximum_fusion.32), channel_id=1, source_target_pairs={{0,16},{16,0},{1,17},{17,1},{2,18},{18,2},{3,19},{19,3},{4,20},{20... | collective-permute-start | bytes 1572872 | tf_op jit(solution)/shard_map/ppermute | solution.py:51
  229.9 142.7 %collective-permute-start.31 = (bf16[128,2560]{1,0:T(8,128)(2,1)}, bf16[128,2560]{1,0:T(8,128)(2,1)}, u32[]{:S(2)}, u32[]{:S(2)}) collective-permute-start(bf16[128,2560]{1,0:T(8,128)(2,1)} %pad_maximum_fusion.21), channel_id=1, source_target_pairs={{0,16},{16,0},{1,17},{17,1},{2,18},{18,2},{3,19},{19,3},{4,20},{20... | collective-permute-start | bytes 1966088 | tf_op jit(solution)/shard_map/ppermute | solution.py:51
  234.0 418.2 %all-reduce.6.cloned.1.call-start = ((), (), s32[]{:S(2)}) async-start(), calls=%async_computation | async-start | bytes 8519680 | tf_op jit(solution)/shard_map/psum | solution.py:354
  237.2 93.5 %collective-permute-start.17 = (bf16[128,2048]{1,0:T(8,128)(2,1)}, bf16[128,2048]{1,0:T(8,128)(2,1)}, u32[]{:S(2)}, u32[]{:S(2)}) collective-permute-start(bf16[128,2048]{1,0:T(8,128)(2,1)} %get-tuple-element.84), channel_id=1, source_target_pairs={{0,2},{2,0},{4,6},{6,4},{8,10},{10,8},{12,14},{14,12},{1,3},{3,1},... | collective-permute-start | bytes 1572872 | tf_op jit(solution)/shard_map/ppermute | solution.py:235
  238.9 91.8 %collective-permute-start.23 = (bf16[128,2048]{1,0:T(8,128)(2,1)}, bf16[128,2048]{1,0:T(8,128)(2,1)}, u32[]{:S(2)}, u32[]{:S(2)}) collective-permute-start(bf16[128,2048]{1,0:T(8,128)(2,1)} %get-tuple-element.85), channel_id=1, source_target_pairs={{0,4},{2,6},{4,0},{6,2},{8,12},{10,14},{12,8},{14,10},{1,5},{3,7},... | collective-permute-start | bytes 1572872 | tf_op jit(solution)/shard_map/ppermute | solution.py:235
  329.2 86.3 %collective-permute-start.36 = (bf16[128,2048]{0,1:T(8,128)(2,1)S(1)}, bf16[128,2048]{0,1:T(8,128)(2,1)}, u32[]{:S(2)}, u32[]{:S(2)}) collective-permute-start(bf16[128,2048]{0,1:T(8,128)(2,1)S(1)} %pad_maximum_fusion.34), channel_id=1, source_target_pairs={{0,16},{16,0},{1,17},{17,1},{2,18},{18,2},{3,19},{19,3},{4,20},{20... | collective-permute-start | bytes 1572872 | tf_op jit(solution)/shard_map/ppermute | solution.py:51
  333.8 24.9 %collective-permute-start.24 = (bf16[64,2048]{1,0:T(8,128)(2,1)S(1)}, bf16[64,2048]{1,0:T(8,128)(2,1)S(1)}, u32[]{:S(2)}, u32[]{:S(2)}) collective-permute-start(bf16[64,2048]{1,0:T(8,128)(2,1)S(1)} %select_convert_fusion.6), channel_id=1, source_target_pairs={{0,8},{2,10},{4,12},{6,14},{8,0},{10,2},{12,4},{14,6},{1,9},{3,11}... | collective-permute-start | bytes 786440 | tf_op jit(solution)/shard_map/ppermute | solution.py:235
  335.5 24.7 %collective-permute-start.18 = (bf16[64,2048]{1,0:T(8,128)(2,1)S(1)}, bf16[64,2048]{1,0:T(8,128)(2,1)S(1)}, u32[]{:S(2)}, u32[]{:S(2)}) collective-permute-start(bf16[64,2048]{1,0:T(8,128)(2,1)S(1)} %select_convert_fusion.7), channel_id=1, source_target_pairs={{0,4},{2,6},{4,0},{6,2},{8,12},{10,14},{12,8},{14,10},{1,5},{3,7},... | collective-permute-start | bytes 786440 | tf_op jit(solution)/shard_map/ppermute | solution.py:235
  370.9 39.6 %collective-permute-start.27 = (bf16[64,2048]{1,0:T(8,128)(2,1)S(1)}, bf16[64,2048]{1,0:T(8,128)(2,1)S(1)}, u32[]{:S(2)}, u32[]{:S(2)}) collective-permute-start(bf16[64,2048]{1,0:T(8,128)(2,1)S(1)} %maximum_select_fusion.9), channel_id=1, source_target_pairs={{0,8},{2,10},{4,12},{6,14},{8,0},{10,2},{12,4},{14,6},{1,9},{3,11}... | collective-permute-start | bytes 786440 | tf_op jit(solution)/shard_map/ppermute | solution.py:235
  384.7 43.3 %collective-permute-start.21 = (bf16[64,2048]{1,0:T(8,128)(2,1)}, bf16[64,2048]{1,0:T(8,128)(2,1)}, u32[]{:S(2)}, u32[]{:S(2)}) collective-permute-start(bf16[64,2048]{1,0:T(8,128)(2,1)} %maximum_select_fusion.8), channel_id=1, source_target_pairs={{0,4},{2,6},{4,0},{6,2},{8,12},{10,14},{12,8},{14,10},{1,5},{3,7},... | collective-permute-start | bytes 786440 | tf_op jit(solution)/shard_map/ppermute | solution.py:235
  411.3 28.4 %collective-permute-start.28 = (bf16[128,2048]{1,0:T(8,128)(2,1)}, bf16[128,2048]{1,0:T(8,128)(2,1)}, u32[]{:S(2)}, u32[]{:S(2)}) collective-permute-start(bf16[128,2048]{1,0:T(8,128)(2,1)} %maximum_select_fusion.5), channel_id=1, source_target_pairs={{0,4},{2,6},{4,0},{6,2},{8,12},{10,14},{12,8},{14,10},{1,5},{3,7},... | collective-permute-start | bytes 1572872 | tf_op jit(solution)/shard_map/ppermute | solution.py:235
  449.4 118.7 %collective-permute-start.29 = (bf16[512,1536]{1,0:T(8,128)(2,1)S(1)}, bf16[512,1536]{1,0:T(8,128)(2,1)}, u32[]{:S(2)}, u32[]{:S(2)}) collective-permute-start(bf16[512,1536]{1,0:T(8,128)(2,1)S(1)} %pad_maximum_fusion.2), channel_id=1, source_target_pairs={{0,16},{1,17},{2,18},{3,19},{4,20},{5,21},{6,22},{7,23},{8,24},{9,... | collective-permute-start | bytes 4718600 | tf_op jit(solution)/shard_map/ppermute | solution.py:358
  462.5 26.5 %collective-permute-start.44 = (bf16[64,2048]{1,0:T(8,128)(2,1)S(1)}, bf16[64,2048]{1,0:T(8,128)(2,1)S(1)}, u32[]{:S(2)}, u32[]{:S(2)}) collective-permute-start(bf16[64,2048]{1,0:T(8,128)(2,1)S(1)} %select_convert_fusion.4), channel_id=1, source_target_pairs={{0,8},{2,10},{4,12},{6,14},{8,0},{10,2},{12,4},{14,6},{1,9},{3,11}... | collective-permute-start | bytes 786440 | tf_op jit(solution)/shard_map/ppermute | solution.py:235
  465.0 25.6 %collective-permute-start.38 = (bf16[64,2048]{1,0:T(8,128)(2,1)S(1)}, bf16[64,2048]{1,0:T(8,128)(2,1)S(1)}, u32[]{:S(2)}, u32[]{:S(2)}) collective-permute-start(bf16[64,2048]{1,0:T(8,128)(2,1)S(1)} %select_convert_fusion.5), channel_id=1, source_target_pairs={{0,4},{2,6},{4,0},{6,2},{8,12},{10,14},{12,8},{14,10},{1,5},{3,7},... | collective-permute-start | bytes 786440 | tf_op jit(solution)/shard_map/ppermute | solution.py:235
  507.9 23.4 %collective-permute-start.40 = (bf16[32,2048]{1,0:T(8,128)(2,1)S(1)}, bf16[32,2048]{1,0:T(8,128)(2,1)S(1)}, u32[]{:S(2)}, u32[]{:S(2)}) collective-permute-start(bf16[32,2048]{1,0:T(8,128)(2,1)S(1)} %add_convert_fusion.5), channel_id=1, source_target_pairs={{0,8},{2,10},{4,12},{6,14},{8,0},{10,2},{12,4},{14,6},{1,9},{3,11}... | collective-permute-start | bytes 393224 | tf_op jit(solution)/shard_map/ppermute | solution.py:235
  508.0 33.6 %collective-permute-start.47 = (bf16[64,2048]{1,0:T(8,128)(2,1)S(1)}, bf16[64,2048]{1,0:T(8,128)(2,1)S(1)}, u32[]{:S(2)}, u32[]{:S(2)}) collective-permute-start(bf16[64,2048]{1,0:T(8,128)(2,1)S(1)} %maximum_select_fusion.11), channel_id=1, source_target_pairs={{0,8},{2,10},{4,12},{6,14},{8,0},{10,2},{12,4},{14,6},{1,9},{3,11}... | collective-permute-start | bytes 786440 | tf_op jit(solution)/shard_map/ppermute | solution.py:235
  541.8 22.9 %collective-permute-start.48 = (bf16[128,2048]{1,0:T(8,128)(2,1)S(1)}, bf16[128,2048]{1,0:T(8,128)(2,1)S(1)}, u32[]{:S(2)}, u32[]{:S(2)}) collective-permute-start(bf16[128,2048]{1,0:T(8,128)(2,1)S(1)} %maximum_select_fusion.7), channel_id=1, source_target_pairs={{0,4},{2,6},{4,0},{6,2},{8,12},{10,14},{12,8},{14,10},{1,5},{3,7},... | collective-permute-start | bytes 1572872 | tf_op jit(solution)/shard_map/ppermute | solution.py:235
  550.0 27.1 %collective-permute-start.14 = (bf16[128,1024]{1,0:T(8,128)(2,1)S(1)}, bf16[128,1024]{1,0:T(8,128)(2,1)S(1)}, u32[]{:S(2)}, u32[]{:S(2)}) collective-permute-start(bf16[128,1024]{1,0:T(8,128)(2,1)S(1)} %get-tuple-element.66), channel_id=1, source_target_pairs={{0,16},{16,0},{1,17},{17,1},{2,18},{18,2},{3,19},{19,3},{4,20},{20... | collective-permute-start | bytes 786440 | tf_op jit(solution)/shard_map/ppermute | solution.py:51
  551.9 22.0 %collective-permute-start.50 = (bf16[256,1024]{1,0:T(8,128)(2,1)S(1)}, bf16[256,1024]{1,0:T(8,128)(2,1)S(1)}, u32[]{:S(2)}, u32[]{:S(2)}) collective-permute-start(bf16[256,1024]{1,0:T(8,128)(2,1)S(1)} %pad_maximum_fusion.35), channel_id=1, source_target_pairs={{0,16},{1,17},{2,18},{3,19},{4,20},{5,21},{6,22},{7,23},{8,24},{9,... | collective-permute-start | bytes 1572872 | tf_op jit(solution)/shard_map/ppermute | solution.py:358
  571.3 88.2 %collective-permute-start.49 = (bf16[512,1536]{1,0:T(8,128)(2,1)}, bf16[512,1536]{1,0:T(8,128)(2,1)}, u32[]{:S(2)}, u32[]{:S(2)}) collective-permute-start(bf16[512,1536]{1,0:T(8,128)(2,1)} %get-tuple-element.57), channel_id=1, source_target_pairs={{16,0},{17,1},{18,2},{19,3},{20,4},{21,5},{22,6},{23,7},{24,8},{25... | collective-permute-start | bytes 4718600 | tf_op jit(solution)/shard_map/ppermute | solution.py:359
  578.3 102.7 %collective-permute-start.54 = (bf16[1024,1024]{1,0:T(8,128)(2,1)}, bf16[1024,1024]{1,0:T(8,128)(2,1)}, u32[]{:S(2)}, u32[]{:S(2)}) collective-permute-start(bf16[1024,1024]{1,0:T(8,128)(2,1)} %get-tuple-element.22), channel_id=1, source_target_pairs={{0,16},{1,17},{2,18},{3,19},{4,20},{5,21},{6,22},{7,23},{8,24},{9,... | collective-permute-start | bytes 6291464 | tf_op jit(solution)/shard_map/ppermute | solution.py:358
  656.1 26.7 %collective-permute-start.53 = (bf16[512,2048]{1,0:T(8,128)(2,1)}, bf16[512,2048]{1,0:T(8,128)(2,1)}, u32[]{:S(2)}, u32[]{:S(2)}) collective-permute-start(bf16[512,2048]{1,0:T(8,128)(2,1)} %get-tuple-element.89), channel_id=1, source_target_pairs={{16,0},{17,1},{18,2},{19,3},{20,4},{21,5},{22,6},{23,7},{24,8},{25... | collective-permute-start | bytes 6291464 | tf_op jit(solution)/shard_map/ppermute | solution.py:359
  (143 other events, 1529.4 us)
Sparse Core Ops, SparseCore 0:
  234.1 196.9 all-reduce.7
  451.1 201.0 all-reduce.5
